TPU v7x, 256 devices: a whole 4x4x8 slice. The times are simulated.
256 devices in a mesh: expert: 8 (over x, core), dp: 8 (over z), pipe: 4 (over y).
Axes of the slice: x: 4, y: 4, z: 8, core: 2. Of those that a mesh axis runs over, the one named last changes fastest.
Arguments:
- tokens: bfloat16 [2048, 3072], P(('expert', 'dp'), 'pipe'), may hold values from -6 to 6
- out_grad: bfloat16 [2048, 3072], P(('expert', 'dp'), 'pipe'), may hold values from -6 to 6
- gate_values: float32 [2048, 2], P(('expert', 'dp')), may hold values from 0.1 to 1
- expert_ids: int32 [2048, 2], P(('expert', 'dp')), may hold values from 0 to 7, all different within a row; in each aligned block of 32 rows (0 to 31, 32 to 63, ...) at most 16 rows name the same one
- w_gate: bfloat16 [8, 3072, 8192], P('expert', None, ('dp', 'pipe')), may hold values from -0.109375 to 0.109375
- w_up: bfloat16 [8, 3072, 8192], P('expert', None, ('dp', 'pipe')), may hold values from -0.109375 to 0.109375
- w_down: bfloat16 [8, 8192, 3072], P('expert', ('dp', 'pipe')), may hold values from -0.0625 to 0.0625
Outputs:
- grad_tokens: bfloat16 [2048, 3072], P(('expert', 'dp'), 'pipe')
- gate_weight_gradient: bfloat16 [8, 3072, 8192], P('expert', None, ('dp', 'pipe'))
- up_weight_gradient: bfloat16 [8, 3072, 8192], P('expert', None, ('dp', 'pipe'))
- grad_down: bfloat16 [8, 8192, 3072], P('expert', ('dp', 'pipe'))
Inputs may be any that keep to these rules, and one draw needn't show every extreme that they name: `expert_ids`: each token names two different experts; among the 32 tokens of one block no expert is named more than 16 times, and in some blocks one is named exactly 16 times.
All inputs are finite; a program needn't handle non-finite values.
Results may differ from a plain program's by a relative error of at most 0.0065.
Values may be sent and summed in bfloat16 or wider, within the bound.
No kernel may reach another device: no remote copies, remote signals or barrier semaphores. Data moves between devices by JAX's collectives and lax.ppermute only.
A program may use at most 128 MiB of HBM per device.

v0:
```python
import functools

import jax
import jax.numpy as jnp
from jax import lax
from jax.experimental import pallas as pl
from jax.experimental.pallas import tpu as pltpu
from jax.sharding import PartitionSpec as P

F32 = jnp.float32
BF16 = jnp.bfloat16
INTERPRET = False
MIB = 1024 * 1024
NN = (((1,), (0,)), ((), ()))
NT = (((1,), (1,)), ((), ()))


def dot(a, b, dims=NN):
    return lax.dot_general(a, b, dims, preferred_element_type=F32)


def dispatch_kernel(expert_count, ids_ref, gates_ref, g_ref, *refs):
    pieces, (sent_ref, slots_ref, picker_ref) = refs[:-3], refs[-3:]
    tokens, feat = g_ref.shape
    capacity = sent_ref.shape[2]
    first, second = ids_ref[0:1, :], ids_ref[1:2, :]
    row = lax.broadcasted_iota(jnp.int32, (tokens, tokens), 0)
    col = lax.broadcasted_iota(jnp.int32, (tokens, tokens), 1)
    tall_first = jnp.sum(jnp.where(row == col, first, 0), axis=1, keepdims=True)
    tall_second = jnp.sum(jnp.where(row == col, second, 0), axis=1, keepdims=True)

    def slot_of(ids):
        same = (tall_first == ids).astype(jnp.int32) + (tall_second == ids).astype(jnp.int32)
        rank = jnp.sum(jnp.where(row < col, same, 0), axis=0, keepdims=True)
        return ids * capacity + rank

    slot_first, slot_second = slot_of(first), slot_of(second)
    slots_ref[0:1, :] = slot_first
    slots_ref[1:2, :] = slot_second
    want = lax.broadcasted_iota(jnp.int32, (expert_count * capacity, tokens), 0)
    hit_first, hit_second = slot_first == want, slot_second == want
    picker = jnp.where(hit_first | hit_second, 1.0, 0.0).astype(BF16)
    picker_ref[...] = picker
    gates = jnp.where(hit_first, gates_ref[0:1, :], 0.0) + jnp.where(
        hit_second, gates_ref[1:2, :], 0.0
    )
    gate = jnp.sum(gates, axis=1, keepdims=True)
    for k, piece in enumerate(pieces):
        rows = dot(picker, piece[...]).astype(BF16)
        sent_ref[:, k] = rows.reshape(expert_count, capacity, feat)
    scaled = (gate * dot(picker, g_ref[...])).astype(BF16)
    sent_ref[:, len(pieces)] = scaled.reshape(expert_count, capacity, feat)


def run_dispatch(ids, gates, out_grad, pieces, expert_count, capacity):
    tokens, feat = out_grad.shape
    here = pl.BlockSpec(memory_space=pltpu.VMEM)
    return pl.pallas_call(
        functools.partial(dispatch_kernel, expert_count),
        in_specs=[here] * (3 + len(pieces)),
        out_specs=[here] * 3,
        out_shape=[
            jax.ShapeDtypeStruct((expert_count, len(pieces) + 1, capacity, feat), BF16),
            jax.ShapeDtypeStruct((2, tokens), jnp.int32),
            jax.ShapeDtypeStruct((expert_count * capacity, tokens), BF16),
        ],
        compiler_params=pltpu.CompilerParams(vmem_limit_bytes=8 * MIB),
        name="dispatch",
        interpret=INTERPRET,
    )(ids, gates, out_grad, *pieces)


def project_kernel(order_ref, x_ref, wg_ref, wu_ref, gate_ref, up_ref):
    groups, pipes, rows, feat = x_ref.shape
    total = groups * rows
    gate = up = None
    for p in range(pipes):
        features = x_ref[:, p].reshape(total, feat)
        cols = pl.ds(pl.multiple_of(order_ref[p] * feat, 128), feat)
        g = dot(features, wg_ref[cols, :])
        u = dot(features, wu_ref[cols, :])
        gate = g if gate is None else gate + g
        up = u if up is None else up + u
    gate_ref[...] = gate
    up_ref[...] = up


def run_project(order, x, wg, wu, step_groups):
    groups, pipes, rows, feat = x.shape
    width, hidden = wg.shape
    step_rows = step_groups * rows
    whole = pl.BlockSpec((width, hidden), lambda s, o: (0, 0))
    result = pl.BlockSpec((step_rows, hidden), lambda s, o: (s, 0))
    return pl.pallas_call(
        project_kernel,
        grid_spec=pltpu.PrefetchScalarGridSpec(
            num_scalar_prefetch=1,
            grid=(groups // step_groups,),
            in_specs=[
                pl.BlockSpec((step_groups, pipes, rows, feat), lambda s, o: (s, 0, 0, 0)),
                whole,
                whole,
            ],
            out_specs=[result, result],
        ),
        out_shape=[jax.ShapeDtypeStruct((groups * rows, hidden), F32)] * 2,
        compiler_params=pltpu.CompilerParams(vmem_limit_bytes=58 * MIB),
        name="project",
        interpret=INTERPRET,
    )(order, x, wg, wu)


def expert_kernel(expert_count, order_ref, gate_ref, up_ref, c0_ref, c1_ref, c3_ref, c2x_ref, c2y_ref, wg_ref, wu_ref, wd_ref, act_ref, gg_ref, ug_ref, ring_ref, cross_ref):
    groups, rows, feat = c0_ref.shape
    pipes = wg_ref.shape[0] // feat
    total = groups * rows
    half = feat // 2
    capacity = rows // expert_count
    early = pl.program_id(0) < pl.num_programs(0) // 2
    opposite = jnp.where(early, c2x_ref[...], c2y_ref[...])
    act_grad = None
    for k, value in enumerate((c0_ref[...], c3_ref[...], opposite, c1_ref[...])):
        cols = pl.ds(pl.multiple_of(order_ref[k] * feat, 128), feat)
        a = dot(value.reshape(total, feat), wd_ref[:, cols], NT)
        act_grad = a if act_grad is None else act_grad + a
    gate = gate_ref[...]
    up = up_ref[...]
    sig = jax.nn.sigmoid(gate)
    linear = gate * sig
    act = (linear * up).astype(BF16)
    gate_grad = (act_grad * up * (sig * (1.0 + gate * (1.0 - sig)))).astype(BF16)
    up_grad = (act_grad * linear).astype(BF16)
    act_ref[...] = act.T
    gg_ref[...] = gate_grad.T
    ug_ref[...] = up_grad.T
    for p in range(pipes):
        cols = slice(p * feat, (p + 1) * feat)
        back = (dot(gate_grad, wg_ref[cols, :], NT) + dot(up_grad, wu_ref[cols, :], NT)).astype(BF16)
        for d in range(groups):
            ring_ref[d, p] = back[d * rows : (d + 1) * rows, :half]
            part = back[d * rows : (d + 1) * rows, half:]
            cross_ref[:, p, d * capacity : (d + 1) * capacity, :] = part.reshape(
                expert_count, capacity, half
            )


def run_expert(order, gate, up, c, wg, wu, wd, expert_count, step_groups):
    groups, rows, feat = c[0].shape
    width, hidden = wg.shape
    pipes = width // feat
    half = feat // 2
    step_rows = step_groups * rows
    step_slots = step_rows // expert_count
    everything = groups * rows
    steps = groups // step_groups
    whole = lambda shape: pl.BlockSpec(shape, lambda s, o: (0, 0))
    flipped = pl.BlockSpec((hidden, step_rows), lambda s, o: (0, s))
    straight = pl.BlockSpec((step_rows, hidden), lambda s, o: (s, 0))
    block = (step_groups, rows, feat)
    piece = pl.BlockSpec(block, lambda s, o: (s, 0, 0))
    return pl.pallas_call(
        functools.partial(expert_kernel, expert_count),
        grid_spec=pltpu.PrefetchScalarGridSpec(
            num_scalar_prefetch=1,
            grid=(steps,),
            in_specs=[
                straight,
                straight,
                piece,
                piece,
                piece,
                pl.BlockSpec(block, lambda s, o: (jnp.minimum(s, steps // 2 - 1), 0, 0)),
                pl.BlockSpec(block, lambda s, o: (jnp.maximum(s - steps // 2, 0), 0, 0)),
                whole((width, hidden)),
                whole((width, hidden)),
                whole((hidden, width)),
            ],
            out_specs=[
                flipped,
                flipped,
                flipped,
                pl.BlockSpec((step_groups, pipes, rows, half), lambda s, o: (s, 0, 0, 0)),
                pl.BlockSpec((expert_count, pipes, step_slots, half), lambda s, o: (0, 0, s, 0)),
            ],
        ),
        out_shape=[jax.ShapeDtypeStruct((hidden, everything), BF16)] * 3
        + [
            jax.ShapeDtypeStruct((groups, pipes, rows, half), BF16),
            jax.ShapeDtypeStruct((expert_count, pipes, everything // expert_count, half), BF16),
        ],
        compiler_params=pltpu.CompilerParams(vmem_limit_bytes=58 * MIB),
        name="expert",
        interpret=INTERPRET,
    )(order, gate, up, *c, wg, wu, wd)


def weight_kernel(order_ref, x_ref, c0_ref, c1_ref, c3_ref, c2x_ref, c2y_ref, act_ref, gg_ref, ug_ref, dwg_ref, dwu_ref, dwd_ref):
    groups, _, rows, feat = x_ref.shape
    step = pl.program_id(0)
    features = x_ref[:, 0].reshape(groups * rows, feat)
    dwg_ref[...] = dot(gg_ref[...], features).astype(BF16).T
    dwu_ref[...] = dot(ug_ref[...], features).astype(BF16).T

    def down(value):
        dwd_ref[...] = dot(act_ref[...], value.reshape(groups * rows, feat)).astype(BF16)

    pl.when(step == 0)(lambda: down(c0_ref[...]))
    pl.when(step == 1)(lambda: down(c3_ref[...]))
    pl.when(step == 2)(lambda: down(jnp.concatenate([c2x_ref[...], c2y_ref[...]], axis=0)))
    pl.when(step == 3)(lambda: down(c1_ref[...]))


def run_weights(order, x, c, act, gg, ug):
    groups, pipes, rows, feat = x.shape
    hidden, everything = act.shape
    whole = pl.BlockSpec((hidden, everything), lambda p, o: (0, 0))
    piece = lambda v: pl.BlockSpec(v.shape, lambda p, o: (0, 0, 0))
    return pl.pallas_call(
        weight_kernel,
        grid_spec=pltpu.PrefetchScalarGridSpec(
            num_scalar_prefetch=1,
            grid=(pipes,),
            in_specs=[pl.BlockSpec((groups, 1, rows, feat), lambda p, o: (0, p, 0, 0))]
            + [piece(v) for v in c]
            + [whole] * 3,
            out_specs=[
                pl.BlockSpec((feat, hidden), lambda p, o: (o[p], 0)),
                pl.BlockSpec((feat, hidden), lambda p, o: (o[p], 0)),
                pl.BlockSpec((hidden, feat), lambda p, o: (0, o[p])),
            ],
        ),
        out_shape=[
            jax.ShapeDtypeStruct((pipes * feat, hidden), BF16),
            jax.ShapeDtypeStruct((pipes * feat, hidden), BF16),
            jax.ShapeDtypeStruct((hidden, pipes * feat), BF16),
        ],
        compiler_params=pltpu.CompilerParams(vmem_limit_bytes=58 * MIB),
        name="weights",
        interpret=INTERPRET,
    )(order, x, *c, act, gg, ug)


def combine_kernel(x_ref, slots_ref, out_ref):
    experts, pipes, slots, half = x_ref.shape
    group_count, _, tokens = slots_ref.shape
    capacity = slots // group_count
    want = lax.broadcasted_iota(jnp.int32, (experts * capacity, tokens), 0)
    for d in range(group_count):
        picked = (slots_ref[d, 0:1, :] == want) | (slots_ref[d, 1:2, :] == want)
        chosen = jnp.where(picked, 1.0, 0.0).astype(BF16)
        for p in range(pipes):
            rows = x_ref[:, p, d * capacity : (d + 1) * capacity, :]
            rows = rows.reshape(experts * capacity, half)
            out_ref[p, d * tokens : (d + 1) * tokens, :] = dot(
                chosen, rows, (((0,), (0,)), ((), ()))
            ).astype(BF16)


def total_of(parts):
    total = parts[0].astype(F32)
    for k in range(1, parts.shape[0]):
        total = total + parts[k].astype(F32)
    return total.astype(BF16)


def run_combine(x, slots):
    _, pipes, _, half = x.shape
    group_count, _, tokens = slots.shape
    here = pl.BlockSpec(memory_space=pltpu.VMEM)
    return pl.pallas_call(
        combine_kernel,
        in_specs=[here, here],
        out_specs=here,
        out_shape=jax.ShapeDtypeStruct((pipes, group_count * tokens, half), BF16),
        compiler_params=pltpu.CompilerParams(vmem_limit_bytes=10 * MIB),
        name="combine",
        interpret=INTERPRET,
    )(x, slots)


def shift(x, axis, by):
    count = lax.axis_size(axis)
    return lax.ppermute(x, axis, [(k, (k + by) % count) for k in range(count)])


def place_kernel(at_ref, *refs):
    pieces, out_ref = refs[:-1], refs[-1]
    count = out_ref.shape[0]
    cut = pieces[-2].shape[0]
    for j in range(count - 1):
        out_ref[at_ref[j]] = pieces[j][...]
    out_ref[at_ref[count - 1], :cut] = pieces[-2][...]
    out_ref[at_ref[count - 1], cut:] = pieces[-1][...]


def groups_ring(x):
    rows, width = x.shape
    cut = rows // 2
    up1, down1 = shift(x, "dp", 1), shift(x, "dp", -1)
    up2, down2 = shift(up1, "dp", 1), shift(down1, "dp", -1)
    up3, down3 = shift(up2, "dp", 1), shift(down2, "dp", -1)
    far_up, far_down = shift(up3[:cut], "dp", 1), shift(down3[cut:], "dp", -1)
    count = lax.axis_size("dp")
    at = (lax.axis_index("dp") + jnp.array([0, 1, 2, 3, 5, 6, 7, 4], jnp.int32)) % count
    here = pl.BlockSpec(memory_space=pltpu.VMEM)
    return pl.pallas_call(
        place_kernel,
        in_specs=[pl.BlockSpec(memory_space=pltpu.SMEM)] + [here] * (count + 1),
        out_specs=here,
        out_shape=jax.ShapeDtypeStruct((count, rows, width), BF16),
        compiler_params=pltpu.CompilerParams(vmem_limit_bytes=6 * MIB),
        name="place",
        interpret=INTERPRET,
    )(at, x, down1, down2, down3, up3, up2, up1, far_up, far_down)


def pipes_ring(x):
    cut = x.shape[0] // 2
    up1, down1 = shift(x, "pipe", 1), shift(x, "pipe", -1)
    far_up, far_down = shift(up1[:cut], "pipe", 1), shift(down1[cut:], "pipe", -1)
    return x, up1, down1, far_up, far_down


def body(tokens, out_grad, gate_values, expert_ids, w_gate, w_up, w_down):
    expert_count = lax.axis_size("expert")
    group_count = lax.axis_size("dp")
    pipe_count = lax.axis_size("pipe")
    token_count, feat = tokens.shape
    capacity = max(token_count // 2, 2 * token_count // expert_count)
    slot_total = expert_count * capacity
    half = feat // 2
    pieces = (tokens, shift(tokens, "pipe", -1), shift(tokens, "pipe", 2), shift(tokens, "pipe", 1))
    sent, slot_index, picker = run_dispatch(
        expert_ids.T, gate_values.T, out_grad, pieces, expert_count, capacity
    )
    received = lax.all_to_all(sent, "expert", split_axis=0, concat_axis=0, tiled=True)
    near = received[:, :pipe_count].transpose(1, 0, 2, 3).reshape(1, pipe_count, slot_total, feat)
    x = lax.all_gather(near, "dp", axis=0, tiled=True)
    c = pipes_ring(groups_ring(received[:, pipe_count].reshape(slot_total, feat)))
    order = (lax.axis_index("pipe") + jnp.arange(pipe_count, dtype=jnp.int32)) % pipe_count
    gate, up = run_project(order, x, w_gate[0], w_up[0], group_count // 4)
    act, gg, ug, ring, cross = run_expert(
        order, gate, up, c, w_gate[0], w_up[0], w_down[0], expert_count, group_count // 4
    )
    over_groups = lax.psum_scatter(
        ring.reshape(group_count, pipe_count * slot_total, half), "dp", scatter_dimension=0, tiled=True
    )
    crossed = lax.all_to_all(cross, "expert", split_axis=0, concat_axis=0, tiled=True)
    late_index, gg = lax.optimization_barrier((slot_index, gg))
    column_slots = lax.all_gather(late_index[None], "dp", axis=0, tiled=True)
    gate_weight_gradient, up_weight_gradient, grad_down = run_weights(order, x, c, act, gg, ug)
    over_groups, column_slots, grad_down = lax.optimization_barrier(
        (over_groups, column_slots, grad_down)
    )
    summed = lax.psum_scatter(
        over_groups.reshape(pipe_count, slot_total, half), "pipe", scatter_dimension=0, tiled=True
    )
    column = run_combine(crossed, column_slots)
    column = lax.all_to_all(column, "pipe", split_axis=0, concat_axis=0, tiled=True)
    column = total_of(column)
    column = lax.all_to_all(
        column.reshape(group_count, token_count, half),
        "dp",
        split_axis=0,
        concat_axis=0,
        tiled=True,
    )
    right = total_of(column)
    returned = lax.all_to_all(
        summed.reshape(expert_count, capacity, half),
        "expert",
        split_axis=0,
        concat_axis=0,
        tiled=True,
    )
    left = jnp.einsum(
        "st,sq->tq", picker, returned.reshape(slot_total, half), preferred_element_type=F32
    ).astype(BF16)
    grad_tokens = jnp.concatenate([left, right], axis=1)
    return (
        grad_tokens,
        gate_weight_gradient[None],
        up_weight_gradient[None],
        grad_down[None],
    )


def solution(mesh):
    rows = P(("expert", "dp"), "pipe")
    pairs = P(("expert", "dp"), None)
    wide = P("expert", None, ("dp", "pipe"))
    tall = P("expert", ("dp", "pipe"), None)

    return jax.shard_map(
        body,
        mesh=mesh,
        in_specs=(rows, rows, pairs, pairs, wide, wide, tall),
        out_specs=(rows, wide, wide, tall),
        check_vma=False,
    )
```

profile of v0, /device:TPU:1, one launch (start us, length us, event | category | flops | bytes accessed | tf_op | source)
XLA Modules:
  0.0 255.2 jit_solution(5668935758077861324)
XLA Ops:
  7.2 3.6 %collective-permute-start = (bf16[32,768]{1,0:T(8,128)(2,1)}, bf16[32,768]{1,0:T(8,128)(2,1)S(1)}, u32[]{:S(2)}, u32[]{:S(2)}) collective-permute-start(bf16[32,768]{1,0:T(8,128)(2,1)} %refs_0_.1), channel_id=1, source_target_pairs={{0,3},{1,0},{2,1},{3,2},{4,7},{5,4},{6,5},{7,6},{8,11},{9,8},{10,9... | collective-permute-start | bytes 147464 | tf_op jit(solution)/shard_map/ppermute | solution.py:283
  12.3 3.2 %collective-permute-done.1.refs_2_ = bf16[32,768]{1,0:T(8,128)(2,1)S(1)} collective-permute-done((bf16[32,768]{1,0:T(8,128)(2,1)}, bf16[32,768]{1,0:T(8,128)(2,1)S(1)}, u32[]{:S(2)}, u32[]{:S(2)}) %collective-permute-start.1) | collective-permute-done | bytes 49184 | tf_op jit(solution)/shard_map/ppermute | solution.py:283
  19.5 20.5 %all_to_all.25 = bf16[8,5,16,768]{3,2,1,0:T(8,128)(2,1)S(1)} all-to-all(bf16[8,5,16,768]{3,2,1,0:T(8,128)(2,1)S(1)} %get-tuple-element.23), channel_id=1, replica_groups=mesh['expert'=8,'dp'=8,'pipe'=4] {'expert'}, dimensions={0} | all-to-all | bytes 1966080 | tf_op jit(solution)/shard_map/all_to_all | solution.py:336
  41.1 1.7 collective-permute-start.6
  42.9 4.0 %collective-permute-start.3 = (bf16[128,768]{1,0:T(8,128)(2,1)S(1)}, bf16[128,768]{1,0:T(8,128)(2,1)S(1)}, u32[]{:S(2)}, u32[]{:S(2)}) collective-permute-start(bf16[128,768]{1,0:T(8,128)(2,1)S(1)} %bitcast.23), channel_id=1, source_target_pairs={{0,28},{4,0},{8,4},{12,8},{16,12},{20,16},{24,20},{28,24},{1,29},{... | collective-permute-start | bytes 589832 | tf_op jit(solution)/shard_map/ppermute | solution.py:283
  46.9 4.2 %collective-permute-done.6.refs_6_ = bf16[128,768]{1,0:T(8,128)(2,1)S(1)} collective-permute-done((bf16[128,768]{1,0:T(8,128)(2,1)S(1)}, bf16[128,768]{1,0:T(8,128)(2,1)S(1)}, u32[]{:S(2)}, u32[]{:S(2)}) %collective-permute-start.6) | collective-permute-done | bytes 196640 | tf_op jit(solution)/shard_map/ppermute | solution.py:283
  51.1 2.7 %collective-permute-start.4 = (bf16[128,768]{1,0:T(8,128)(2,1)S(1)}, bf16[128,768]{1,0:T(8,128)(2,1)S(1)}, u32[]{:S(2)}, u32[]{:S(2)}) collective-permute-start(bf16[128,768]{1,0:T(8,128)(2,1)S(1)} %collective-permute-done.3.refs_1_), channel_id=1, source_target_pairs={{0,28},{4,0},{8,4},{12,8},{16,12},{20,16},{24,20},{28,24},{1,29},{... | collective-permute-start | bytes 589832 | tf_op jit(solution)/shard_map/ppermute | solution.py:283
  53.8 6.3 %collective-permute-done.7.refs_5_ = bf16[128,768]{1,0:T(8,128)(2,1)S(1)} collective-permute-done((bf16[128,768]{1,0:T(8,128)(2,1)S(1)}, bf16[128,768]{1,0:T(8,128)(2,1)S(1)}, u32[]{:S(2)}, u32[]{:S(2)}) %collective-permute-start.7) | collective-permute-done | bytes 196640 | tf_op jit(solution)/shard_map/ppermute | solution.py:283
  60.2 1.9 collective-permute-done.4.refs_2_
  62.1 3.5 %collective-permute-start.5 = (bf16[128,768]{1,0:T(8,128)(2,1)S(1)}, bf16[128,768]{1,0:T(8,128)(2,1)S(1)}, u32[]{:S(2)}, u32[]{:S(2)}) collective-permute-start(bf16[128,768]{1,0:T(8,128)(2,1)S(1)} %collective-permute-done.4.refs_2_), channel_id=1, source_target_pairs={{0,28},{4,0},{8,4},{12,8},{16,12},{20,16},{24,20},{28,24},{1,29},{... | collective-permute-start | bytes 589832 | tf_op jit(solution)/shard_map/ppermute | solution.py:283
  65.6 5.6 %collective-permute-done.8.refs_4_ = bf16[128,768]{1,0:T(8,128)(2,1)S(1)} collective-permute-done((bf16[128,768]{1,0:T(8,128)(2,1)S(1)}, bf16[128,768]{1,0:T(8,128)(2,1)S(1)}, u32[]{:S(2)}, u32[]{:S(2)}) %collective-permute-start.8) | collective-permute-done | bytes 196640 | tf_op jit(solution)/shard_map/ppermute | solution.py:283
  71.3 2.4 collective-permute-done.5.refs_3_
  73.7 3.6 %collective-permute-start.10 = (bf16[64,768]{1,0:T(8,128)(2,1)S(1)}, bf16[64,768]{1,0:T(8,128)(2,1)S(1)}, u32[]{:S(2)}, u32[]{:S(2)}) collective-permute-start(bf16[64,768]{1,0:T(8,128)(2,1)S(1)} %slice.75), channel_id=1, source_target_pairs={{0,28},{4,0},{8,4},{12,8},{16,12},{20,16},{24,20},{28,24},{1,29},{... | collective-permute-start | bytes 294920 | tf_op jit(solution)/shard_map/ppermute | solution.py:283
  77.3 1.3 collective-permute-done.9.refs_7_
  78.6 2.5 collective-permute-done.10.refs_8_
  81.9 2.7 %collective-permute-start.12 = (bf16[8,128,768]{2,1,0:T(8,128)(2,1)S(1)}, bf16[8,128,768]{2,1,0:T(8,128)(2,1)S(1)}, u32[]{:S(2)}, u32[]{:S(2)}) collective-permute-start(bf16[8,128,768]{2,1,0:T(8,128)(2,1)S(1)} %place.1.c0_ref), channel_id=1, source_target_pairs={{0,3},{1,0},{2,1},{3,2},{4,7},{5,4},{6,5},{7,6},{8,11},{9,8},{10,9... | collective-permute-start | bytes 4718600 | tf_op jit(solution)/shard_map/ppermute | solution.py:283
  84.5 30.6 %collective-permute-done.11.c1_ref = bf16[8,128,768]{2,1,0:T(8,128)(2,1)S(1)} collective-permute-done((bf16[8,128,768]{2,1,0:T(8,128)(2,1)S(1)}, bf16[8,128,768]{2,1,0:T(8,128)(2,1)S(1)}, u32[]{:S(2)}, u32[]{:S(2)}) %collective-permute-start.11) | collective-permute-done | bytes 1572896 | tf_op jit(solution)/shard_map/ppermute | solution.py:283
  115.3 1.2 copy-done.6
  116.8 2.6 %collective-permute-start.14 = (bf16[4,128,768]{2,1,0:T(8,128)(2,1)S(1)}, bf16[4,128,768]{2,1,0:T(8,128)(2,1)}, u32[]{:S(2)}, u32[]{:S(2)}) collective-permute-start(bf16[4,128,768]{2,1,0:T(8,128)(2,1)S(1)} %slice.77), channel_id=1, source_target_pairs={{0,3},{1,0},{2,1},{3,2},{4,7},{5,4},{6,5},{7,6},{8,11},{9,8},{10,9... | collective-permute-start | bytes 2359304 | tf_op jit(solution)/shard_map/ppermute | solution.py:283
  120.0 5.0 %all-gather.4.cloned.1.call-done.x_ref = bf16[8,4,128,768]{3,2,1,0:T(8,128)(2,1)} async-done(((bf16[1,4,128,768]{3,2,1,0:T(8,128)(2,1)}), bf16[8,4,128,768]{3,2,1,0:T(8,128)(2,1)}) %all-gather.4.cloned.1.call-update) | async-done | bytes 6291472 | tf_op jit(solution)/shard_map/all_gather | solution.py:338
  124.9 8.5 %project.1 = (f32[1024,256]{1,0:T(8,128)}, f32[1024,256]{1,0:T(8,128)}) custom-call(s32[4]{0:T(128)} %and_select_fusion.1.order_ref, bf16[8,4,128,768]{3,2,1,0:T(8,128)(2,1)} %all-gather.4.cloned.1.call-done.x_ref, bf16[3072,256]{1,0:T(8,128)(2,1)} %bitcast.28, bf16[3072,256]{1,0:T(8,128)(2,1)} %bitcast.30), custom_call_target="tpu_custom_call" | custom-call | tf_op jit(solution)/shard_map/project/pallas_call | solution.py:94
  133.5 14.9 %expert.1 = (bf16[256,1024]{1,0:T(8,128)(2,1)}, bf16[256,1024]{1,0:T(8,128)(2,1)}, bf16[256,1024]{1,0:T(8,128)(2,1)}, bf16[8,4,128,384]{3,2,1,0:T(8,128)(2,1)}, bf16[8,4,128,384]{3,2,1,0:T(8,128)(2,1)}) custom-call(s32[4]{0:T(128)} %and_select_fusion.1.order_ref, f32[1024,256]{1,0:T(8,128)} %get-tuple-element.24.gate_ref, ...), custom_call_target="tpu_custom_call" | custom-call | tf_op jit(solution)/shard_map/expert/pallas_call | solution.py:161
  148.4 7.3 %all-to-all-start.2 = ((bf16[8,4,128,384]{3,2,1,0:T(8,128)(2,1)}), bf16[8,4,128,384]{3,2,1,0:T(8,128)(2,1)S(1)}, u32[]{:S(2)}, u32[]{:S(2)}) async-start(bf16[8,4,128,384]{3,2,1,0:T(8,128)(2,1)} %get-tuple-element.35), calls=%async_computation.4 | async-start | bytes 6291456 | tf_op jit(solution)/shard_map/all_to_all | solution.py:348
  155.7 12.3 %weights.1 = (bf16[3072,256]{1,0:T(8,128)(2,1)}, bf16[3072,256]{1,0:T(8,128)(2,1)}, bf16[256,3072]{1,0:T(8,128)(2,1)}) custom-call(s32[4]{0:T(128)} %and_select_fusion.1.order_ref, bf16[8,4,128,768]{3,2,1,0:T(8,128)(2,1)} %all-gather.4.cloned.1.call-done.x_ref, bf16[8,128,768]{2,1,0:T(8,128)(2,1)} %copy-done, bf16[8,128,768]{2,1,0:T(8,128)(2,1)} %copy-done.5, ...), custom_call_target="tpu_custom_call" | custom-call | tf_op jit(solution)/shard_map/weights/pallas_call | solution.py:218
  167.9 15.1 %all-gather.1.slots_ref = s32[8,2,32]{2,1,0:T(2,128)S(1)} all-gather(s32[1,2,32]{2,1,0:T(2,128)S(1)} %bitcast.27), channel_id=2, replica_groups=mesh['expert'=8,'dp'=8,'pipe'=4] {'dp'}, dimensions={0}, use_global_device_ids=true | all-gather | bytes 2304 | tf_op jit(solution)/shard_map/all_gather | solution.py:350
  183.0 10.7 %reduce-scatter.3.cloned.1.call-done = bf16[1,512,384]{2,1,0:T(8,128)(2,1)} async-done(((bf16[8,512,384]{2,1,0:T(8,128)(2,1)}), bf16[1,512,384]{2,1,0:T(8,128)(2,1)}) %reduce-scatter.3.cloned.1.call-update) | async-done | bytes 393232 | tf_op jit(solution)/shard_map/reduce_scatter | solution.py:345
  194.4 12.3 %all_to_all.26 = bf16[4,256,384]{2,1,0:T(8,128)(2,1)S(1)} all-to-all(bf16[4,256,384]{2,1,0:T(8,128)(2,1)S(1)} %combine.1), channel_id=1, replica_groups=mesh['expert'=8,'dp'=8,'pipe'=4] {'pipe'}, dimensions={0} | all-to-all | bytes 1572864 | tf_op jit(solution)/shard_map/all_to_all | solution.py:359
  206.8 13.3 %reduce-scatter.5.cloned.1.call-done = bf16[1,128,384]{2,1,0:T(8,128)(2,1)} async-done(((bf16[4,128,384]{2,1,0:T(8,128)(2,1)}), bf16[1,128,384]{2,1,0:T(8,128)(2,1)}) %reduce-scatter.5.cloned.1.call-update) | async-done | bytes 98320 | tf_op jit(solution)/shard_map/reduce_scatter | solution.py:355
  220.1 7.4 %all-to-all-start.1 = ((bf16[8,16,384]{2,1,0:T(8,128)(2,1)}), bf16[8,16,384]{2,1,0:T(8,128)(2,1)S(1)}, u32[]{:S(2)}, u32[]{:S(2)}) async-start(bf16[8,16,384]{2,1,0:T(8,128)(2,1)} %bitcast.37), calls=%async_computation.3 | async-start | bytes 196608 | tf_op jit(solution)/shard_map/all_to_all | solution.py:369
  228.2 4.2 %all-to-all-done.1 = bf16[8,16,384]{2,1,0:T(8,128)(2,1)S(1)} async-done(((bf16[8,16,384]{2,1,0:T(8,128)(2,1)}), bf16[8,16,384]{2,1,0:T(8,128)(2,1)S(1)}, u32[]{:S(2)}, u32[]{:S(2)}) %all-to-all-start.1) | async-done | bytes 98336 | tf_op jit(solution)/shard_map/all_to_all | solution.py:369
  232.4 6.7 %all-to-all-start.4 = ((bf16[8,32,384]{2,1,0:T(8,128)(2,1)}), bf16[8,32,384]{2,1,0:T(8,128)(2,1)S(1)}, u32[]{:S(2)}, u32[]{:S(2)}) async-start(bf16[8,32,384]{2,1,0:T(8,128)(2,1)} %bitcast.13), calls=%async_computation.6 | async-start | bytes 393216 | tf_op jit(solution)/shard_map/all_to_all | solution.py:361
  239.3 8.8 %all-to-all-done.4 = bf16[8,32,384]{2,1,0:T(8,128)(2,1)S(1)} async-done(((bf16[8,32,384]{2,1,0:T(8,128)(2,1)}), bf16[8,32,384]{2,1,0:T(8,128)(2,1)S(1)}, u32[]{:S(2)}, u32[]{:S(2)}) %all-to-all-start.4) | async-done | bytes 196640 | tf_op jit(solution)/shard_map/all_to_all | solution.py:361
  (51 shorter events, 10.7 us)
Async XLA Ops:
  7.2 117.8 %all-gather.4.cloned.1.call-start = ((), (), s32[]{:S(2)}) async-start(), calls=%async_computation.7 | async-start | bytes 7077888 | tf_op jit(solution)/shard_map/all_gather | solution.py:338
  7.2 5.1 %collective-permute-start = (bf16[32,768]{1,0:T(8,128)(2,1)}, bf16[32,768]{1,0:T(8,128)(2,1)S(1)}, u32[]{:S(2)}, u32[]{:S(2)}) collective-permute-start(bf16[32,768]{1,0:T(8,128)(2,1)} %refs_0_.1), channel_id=1, source_target_pairs={{0,3},{1,0},{2,1},{3,2},{4,7},{5,4},{6,5},{7,6},{8,11},{9,8},{10,9... | collective-permute-start | bytes 147464 | tf_op jit(solution)/shard_map/ppermute | solution.py:283
  10.8 4.7 %collective-permute-start.1 = (bf16[32,768]{1,0:T(8,128)(2,1)}, bf16[32,768]{1,0:T(8,128)(2,1)S(1)}, u32[]{:S(2)}, u32[]{:S(2)}) collective-permute-start(bf16[32,768]{1,0:T(8,128)(2,1)} %refs_0_.1), channel_id=1, source_target_pairs={{0,2},{1,3},{2,0},{3,1},{4,6},{5,7},{6,4},{7,5},{8,10},{9,11},{10,... | collective-permute-start | bytes 147464 | tf_op jit(solution)/shard_map/ppermute | solution.py:283
  11.2 4.8 %collective-permute-start.2 = (bf16[32,768]{1,0:T(8,128)(2,1)}, bf16[32,768]{1,0:T(8,128)(2,1)S(1)}, u32[]{:S(2)}, u32[]{:S(2)}) collective-permute-start(bf16[32,768]{1,0:T(8,128)(2,1)} %refs_0_.1), channel_id=1, source_target_pairs={{0,1},{1,2},{2,3},{3,0},{4,5},{5,6},{6,7},{7,4},{8,9},{9,10},{10,1... | collective-permute-start | bytes 147464 | tf_op jit(solution)/shard_map/ppermute | solution.py:283
  16.0 0.8 copy-start.1
  16.8 0.8 copy-start.2
  17.6 0.7 copy-start.3
  18.3 0.7 copy-start.4
  40.1 37.2 %copy-start.7 = (s32[8]{0:T(128)S(1)}, s32[8]{0:T(128)}, u32[]{:S(2)}) copy-start(s32[8]{0:T(128)} %constant.40.clone) | copy-start | bytes 100
  41.1 152.6 %reduce-scatter.3.cloned.1.call-start = ((), (), s32[]{:S(2)}) async-start(), calls=%async_computation.8 | async-start | bytes 3538944 | tf_op jit(solution)/shard_map/reduce_scatter | solution.py:345
  41.1 10.0 %collective-permute-start.6 = (bf16[128,768]{1,0:T(8,128)(2,1)S(1)}, bf16[128,768]{1,0:T(8,128)(2,1)S(1)}, u32[]{:S(2)}, u32[]{:S(2)}) collective-permute-start(bf16[128,768]{1,0:T(8,128)(2,1)S(1)} %bitcast.22), channel_id=1, source_target_pairs={{0,4},{4,8},{8,12},{12,16},{16,20},{20,24},{24,28},{28,0},{1,5},{5... | collective-permute-start | bytes 589832 | tf_op jit(solution)/shard_map/ppermute | solution.py:283
  42.9 8.3 %collective-permute-start.3 = (bf16[128,768]{1,0:T(8,128)(2,1)S(1)}, bf16[128,768]{1,0:T(8,128)(2,1)S(1)}, u32[]{:S(2)}, u32[]{:S(2)}) collective-permute-start(bf16[128,768]{1,0:T(8,128)(2,1)S(1)} %bitcast.23), channel_id=1, source_target_pairs={{0,28},{4,0},{8,4},{12,8},{16,12},{20,16},{24,20},{28,24},{1,29},{... | collective-permute-start | bytes 589832 | tf_op jit(solution)/shard_map/ppermute | solution.py:283
  51.1 9.0 %collective-permute-start.7 = (bf16[128,768]{1,0:T(8,128)(2,1)S(1)}, bf16[128,768]{1,0:T(8,128)(2,1)S(1)}, u32[]{:S(2)}, u32[]{:S(2)}) collective-permute-start(bf16[128,768]{1,0:T(8,128)(2,1)S(1)} %collective-permute-done.6.refs_6_), channel_id=1, source_target_pairs={{0,4},{4,8},{8,12},{12,16},{16,20},{20,24},{24,28},{28,0},{1,5},{5... | collective-permute-start | bytes 589832 | tf_op jit(solution)/shard_map/ppermute | solution.py:283
  51.1 11.0 %collective-permute-start.4 = (bf16[128,768]{1,0:T(8,128)(2,1)S(1)}, bf16[128,768]{1,0:T(8,128)(2,1)S(1)}, u32[]{:S(2)}, u32[]{:S(2)}) collective-permute-start(bf16[128,768]{1,0:T(8,128)(2,1)S(1)} %collective-permute-done.3.refs_1_), channel_id=1, source_target_pairs={{0,28},{4,0},{8,4},{12,8},{16,12},{20,16},{24,20},{28,24},{1,29},{... | collective-permute-start | bytes 589832 | tf_op jit(solution)/shard_map/ppermute | solution.py:283
  60.1 11.1 %collective-permute-start.8 = (bf16[128,768]{1,0:T(8,128)(2,1)S(1)}, bf16[128,768]{1,0:T(8,128)(2,1)S(1)}, u32[]{:S(2)}, u32[]{:S(2)}) collective-permute-start(bf16[128,768]{1,0:T(8,128)(2,1)S(1)} %collective-permute-done.7.refs_5_), channel_id=1, source_target_pairs={{0,4},{4,8},{8,12},{12,16},{16,20},{20,24},{24,28},{28,0},{1,5},{5... | collective-permute-start | bytes 589832 | tf_op jit(solution)/shard_map/ppermute | solution.py:283
  62.1 11.6 %collective-permute-start.5 = (bf16[128,768]{1,0:T(8,128)(2,1)S(1)}, bf16[128,768]{1,0:T(8,128)(2,1)S(1)}, u32[]{:S(2)}, u32[]{:S(2)}) collective-permute-start(bf16[128,768]{1,0:T(8,128)(2,1)S(1)} %collective-permute-done.4.refs_2_), channel_id=1, source_target_pairs={{0,28},{4,0},{8,4},{12,8},{16,12},{20,16},{24,20},{28,24},{1,29},{... | collective-permute-start | bytes 589832 | tf_op jit(solution)/shard_map/ppermute | solution.py:283
  71.2 7.4 %collective-permute-start.9 = (bf16[64,768]{1,0:T(8,128)(2,1)S(1)}, bf16[64,768]{1,0:T(8,128)(2,1)S(1)}, u32[]{:S(2)}, u32[]{:S(2)}) collective-permute-start(bf16[64,768]{1,0:T(8,128)(2,1)S(1)} %slice.74), channel_id=1, source_target_pairs={{0,4},{4,8},{8,12},{12,16},{16,20},{20,24},{24,28},{28,0},{1,5},{5... | collective-permute-start | bytes 294920 | tf_op jit(solution)/shard_map/ppermute | solution.py:283
  73.7 7.4 %collective-permute-start.10 = (bf16[64,768]{1,0:T(8,128)(2,1)S(1)}, bf16[64,768]{1,0:T(8,128)(2,1)S(1)}, u32[]{:S(2)}, u32[]{:S(2)}) collective-permute-start(bf16[64,768]{1,0:T(8,128)(2,1)S(1)} %slice.75), channel_id=1, source_target_pairs={{0,28},{4,0},{8,4},{12,8},{16,12},{20,16},{24,20},{28,24},{1,29},{... | collective-permute-start | bytes 294920 | tf_op jit(solution)/shard_map/ppermute | solution.py:283
  81.8 34.9 %copy-start = (bf16[8,128,768]{2,1,0:T(8,128)(2,1)}, bf16[8,128,768]{2,1,0:T(8,128)(2,1)S(1)}, u32[]{:S(2)}) copy-start(bf16[8,128,768]{2,1,0:T(8,128)(2,1)S(1)} %place.1.c0_ref) | copy-start | bytes 4718596
  81.8 33.4 %collective-permute-start.11 = (bf16[8,128,768]{2,1,0:T(8,128)(2,1)S(1)}, bf16[8,128,768]{2,1,0:T(8,128)(2,1)S(1)}, u32[]{:S(2)}, u32[]{:S(2)}) collective-permute-start(bf16[8,128,768]{2,1,0:T(8,128)(2,1)S(1)} %place.1.c0_ref), channel_id=1, source_target_pairs={{0,1},{1,2},{2,3},{3,0},{4,5},{5,6},{6,7},{7,4},{8,9},{9,10},{10,1... | collective-permute-start | bytes 4718600 | tf_op jit(solution)/shard_map/ppermute | solution.py:283
  81.9 33.4 %collective-permute-start.12 = (bf16[8,128,768]{2,1,0:T(8,128)(2,1)S(1)}, bf16[8,128,768]{2,1,0:T(8,128)(2,1)S(1)}, u32[]{:S(2)}, u32[]{:S(2)}) collective-permute-start(bf16[8,128,768]{2,1,0:T(8,128)(2,1)S(1)} %place.1.c0_ref), channel_id=1, source_target_pairs={{0,3},{1,0},{2,1},{3,2},{4,7},{5,4},{6,5},{7,6},{8,11},{9,8},{10,9... | collective-permute-start | bytes 4718600 | tf_op jit(solution)/shard_map/ppermute | solution.py:283
  115.2 1.6 copy-start.5
  115.2 18.2 %collective-permute-start.13 = (bf16[4,128,768]{2,1,0:T(8,128)(2,1)S(1)}, bf16[4,128,768]{2,1,0:T(8,128)(2,1)}, u32[]{:S(2)}, u32[]{:S(2)}) collective-permute-start(bf16[4,128,768]{2,1,0:T(8,128)(2,1)S(1)} %slice.76), channel_id=1, source_target_pairs={{0,1},{1,2},{2,3},{3,0},{4,5},{5,6},{6,7},{7,4},{8,9},{9,10},{10,1... | collective-permute-start | bytes 2359304 | tf_op jit(solution)/shard_map/ppermute | solution.py:283
  115.3 1.3 copy-start.6
  116.8 16.7 %collective-permute-start.14 = (bf16[4,128,768]{2,1,0:T(8,128)(2,1)S(1)}, bf16[4,128,768]{2,1,0:T(8,128)(2,1)}, u32[]{:S(2)}, u32[]{:S(2)}) collective-permute-start(bf16[4,128,768]{2,1,0:T(8,128)(2,1)S(1)} %slice.77), channel_id=1, source_target_pairs={{0,3},{1,0},{2,1},{3,2},{4,7},{5,4},{6,5},{7,6},{8,11},{9,8},{10,9... | collective-permute-start | bytes 2359304 | tf_op jit(solution)/shard_map/ppermute | solution.py:283
  148.4 45.3 %all-to-all-start.2 = ((bf16[8,4,128,384]{3,2,1,0:T(8,128)(2,1)}), bf16[8,4,128,384]{3,2,1,0:T(8,128)(2,1)S(1)}, u32[]{:S(2)}, u32[]{:S(2)}) async-start(bf16[8,4,128,384]{3,2,1,0:T(8,128)(2,1)} %get-tuple-element.35), calls=%async_computation.4 | async-start | bytes 6291456 | tf_op jit(solution)/shard_map/all_to_all | solution.py:348
  155.7 64.4 %reduce-scatter.5.cloned.1.call-start = ((), (), s32[]{:S(2)}) async-start(), calls=%async_computation.9 | async-start | bytes 491520 | tf_op jit(solution)/shard_map/reduce_scatter | solution.py:355
  220.1 12.3 %all-to-all-start.1 = ((bf16[8,16,384]{2,1,0:T(8,128)(2,1)}), bf16[8,16,384]{2,1,0:T(8,128)(2,1)S(1)}, u32[]{:S(2)}, u32[]{:S(2)}) async-start(bf16[8,16,384]{2,1,0:T(8,128)(2,1)} %bitcast.37), calls=%async_computation.3 | async-start | bytes 196608 | tf_op jit(solution)/shard_map/all_to_all | solution.py:369
  232.4 15.7 %all-to-all-start.4 = ((bf16[8,32,384]{2,1,0:T(8,128)(2,1)}), bf16[8,32,384]{2,1,0:T(8,128)(2,1)S(1)}, u32[]{:S(2)}, u32[]{:S(2)}) async-start(bf16[8,32,384]{2,1,0:T(8,128)(2,1)} %bitcast.13), calls=%async_computation.6 | async-start | bytes 393216 | tf_op jit(solution)/shard_map/all_to_all | solution.py:361
Sparse Core Ops, SparseCore 0:
  41.2 83.6 all-gather.3
  148.5 45.1 reduce-scatter.2
  196.2 23.7 reduce-scatter.4
where the time goes:
time: 256 us; the launch traced here: 255 us
  waiting for transfers between devices  101 us (39%)
  blocking collectives  47.9 us (19%)
  starting transfers between devices  47.2 us (18%)
  Pallas kernels  37.5 us (15%)
  between operations  13.9 us (5%)
  local copies, waits for them, and re-layouts  5.52 us (2%)
    ppermute x15, waiting for transfers between devices, shift(): return lax.ppermute(x, axis, [(k, (k + by) % count) for k in range(count)])  59.1 us
    ppermute x15, starting transfers between devices, shift(): return lax.ppermute(x, axis, [(k, (k + by) % count) for k in range(count)])  25.8 us
    all_to_all x1, blocking collectives, body(): lax.all_to_all(sent, 'expert', split_axis=0, concat_axis=0, tiled=True)  20.5 us
    all_gather x1, blocking collectives, body(): column_slots = lax.all_gather(late_index[None], 'dp', axis=0, tiled=True)  15.1 us
    pallas_call x1, Pallas kernels, run_expert(): pl.pallas_call(functools.partial(expert_kernel, expert_count), grid_spec=...  14.9 us
    reduce_scatter x1, waiting for transfers between devices, body(): lax.psum_scatter(over_groups.reshape(pipe_count, slot_total, half), 'pipe...  13.3 us
    all_to_all x1, blocking collectives, body(): lax.all_to_all(column, 'pipe', split_axis=0, concat_axis=0, tiled=True)  12.3 us
    pallas_call x1, Pallas kernels, run_weights(): pl.pallas_call(weight_kernel, grid_spec=pltpu.PrefetchScalarGridSpec(num_...  12.3 us
  transfers between devices with their start and end apart: 21, of which 16 were waited for; matrix products, arithmetic and copies ran while one was open for 1% of the time, Pallas kernels for 9%

commit v1 on v0

--- a/solution.py
+++ b/solution.py
@@ -7,12 +7,14 @@
 from jax.experimental.pallas import tpu as pltpu
 from jax.sharding import PartitionSpec as P
 
+
 F32 = jnp.float32
 BF16 = jnp.bfloat16
 INTERPRET = False
 MIB = 1024 * 1024
 NN = (((1,), (0,)), ((), ()))
 NT = (((1,), (1,)), ((), ()))
+TN = (((0,), (0,)), ((), ()))
 
 
 def dot(a, b, dims=NN):
@@ -64,19 +66,25 @@
             jax.ShapeDtypeStruct((2, tokens), jnp.int32),
             jax.ShapeDtypeStruct((expert_count * capacity, tokens), BF16),
         ],
-        compiler_params=pltpu.CompilerParams(vmem_limit_bytes=8 * MIB),
+        compiler_params=pltpu.CompilerParams(vmem_limit_bytes=58 * MIB),
         name="dispatch",
         interpret=INTERPRET,
     )(ids, gates, out_grad, *pieces)
 
 
-def project_kernel(order_ref, x_ref, wg_ref, wu_ref, gate_ref, up_ref):
-    groups, pipes, rows, feat = x_ref.shape
-    total = groups * rows
+def in_order(pieces, early):
+    own, before, after, far_early, far_late = pieces
+    return own[...], after[...], jnp.where(early, far_early[...], far_late[...]), before[...]
+
+
+def project_kernel(order_ref, *refs):
+    pieces, (wg_ref, wu_ref, gate_ref, up_ref) = refs[:5], refs[5:]
+    groups, rows, feat = pieces[0].shape
+    early = pl.program_id(0) < pl.num_programs(0) // 2
     gate = up = None
-    for p in range(pipes):
-        features = x_ref[:, p].reshape(total, feat)
-        cols = pl.ds(pl.multiple_of(order_ref[p] * feat, 128), feat)
+    for k, value in enumerate(in_order(pieces, early)):
+        features = value.reshape(groups * rows, feat)
+        cols = pl.ds(pl.multiple_of(order_ref[k] * feat, 128), feat)
         g = dot(features, wg_ref[cols, :])
         u = dot(features, wu_ref[cols, :])
         gate = g if gate is None else gate + g
@@ -85,19 +93,26 @@
     up_ref[...] = up
 
 
-def run_project(order, x, wg, wu, step_groups):
-    groups, pipes, rows, feat = x.shape
+def run_project(order, c, wg, wu, step_groups):
+    groups, rows, feat = c[0].shape
     width, hidden = wg.shape
+    steps = groups // step_groups
     step_rows = step_groups * rows
+    block = (step_groups, rows, feat)
+    piece = pl.BlockSpec(block, lambda s, o: (s, 0, 0))
     whole = pl.BlockSpec((width, hidden), lambda s, o: (0, 0))
     result = pl.BlockSpec((step_rows, hidden), lambda s, o: (s, 0))
     return pl.pallas_call(
         project_kernel,
         grid_spec=pltpu.PrefetchScalarGridSpec(
             num_scalar_prefetch=1,
-            grid=(groups // step_groups,),
+            grid=(steps,),
             in_specs=[
-                pl.BlockSpec((step_groups, pipes, rows, feat), lambda s, o: (s, 0, 0, 0)),
+                piece,
+                piece,
+                piece,
+                pl.BlockSpec(block, lambda s, o: (jnp.minimum(s, steps // 2 - 1), 0, 0)),
+                pl.BlockSpec(block, lambda s, o: (jnp.maximum(s - steps // 2, 0), 0, 0)),
                 whole,
                 whole,
             ],
@@ -107,32 +122,28 @@
         compiler_params=pltpu.CompilerParams(vmem_limit_bytes=58 * MIB),
         name="project",
         interpret=INTERPRET,
-    )(order, x, wg, wu)
-
-
-def expert_kernel(expert_count, order_ref, gate_ref, up_ref, c0_ref, c1_ref, c3_ref, c2x_ref, c2y_ref, wg_ref, wu_ref, wd_ref, act_ref, gg_ref, ug_ref, ring_ref, cross_ref):
-    groups, rows, feat = c0_ref.shape
-    pipes = wg_ref.shape[0] // feat
+    )(order, *c, wg, wu)
+
+
+def expert_kernel(expert_count, order_ref, gate_ref, up_ref, x_ref, wg_ref, wu_ref, wd_ref, act_ref, gg_ref, ug_ref, ring_ref, cross_ref):
+    groups, pipes, rows, feat = x_ref.shape
     total = groups * rows
     half = feat // 2
     capacity = rows // expert_count
-    early = pl.program_id(0) < pl.num_programs(0) // 2
-    opposite = jnp.where(early, c2x_ref[...], c2y_ref[...])
     act_grad = None
-    for k, value in enumerate((c0_ref[...], c3_ref[...], opposite, c1_ref[...])):
+    for k in range(pipes):
         cols = pl.ds(pl.multiple_of(order_ref[k] * feat, 128), feat)
-        a = dot(value.reshape(total, feat), wd_ref[:, cols], NT)
+        a = dot(x_ref[:, k].reshape(total, feat), wd_ref[:, cols], NT)
         act_grad = a if act_grad is None else act_grad + a
     gate = gate_ref[...]
     up = up_ref[...]
     sig = jax.nn.sigmoid(gate)
     linear = gate * sig
-    act = (linear * up).astype(BF16)
     gate_grad = (act_grad * up * (sig * (1.0 + gate * (1.0 - sig)))).astype(BF16)
     up_grad = (act_grad * linear).astype(BF16)
-    act_ref[...] = act.T
-    gg_ref[...] = gate_grad.T
-    ug_ref[...] = up_grad.T
+    act_ref[...] = (linear * up).astype(BF16)
+    gg_ref[...] = gate_grad
+    ug_ref[...] = up_grad
     for p in range(pipes):
         cols = slice(p * feat, (p + 1) * feat)
         back = (dot(gate_grad, wg_ref[cols, :], NT) + dot(up_grad, wu_ref[cols, :], NT)).astype(BF16)
@@ -144,46 +155,37 @@
             )
 
 
-def run_expert(order, gate, up, c, wg, wu, wd, expert_count, step_groups):
-    groups, rows, feat = c[0].shape
+def run_expert(order, gate, up, x, wg, wu, wd, expert_count, step_groups):
+    groups, pipes, rows, feat = x.shape
     width, hidden = wg.shape
-    pipes = width // feat
     half = feat // 2
     step_rows = step_groups * rows
     step_slots = step_rows // expert_count
     everything = groups * rows
-    steps = groups // step_groups
     whole = lambda shape: pl.BlockSpec(shape, lambda s, o: (0, 0))
-    flipped = pl.BlockSpec((hidden, step_rows), lambda s, o: (0, s))
     straight = pl.BlockSpec((step_rows, hidden), lambda s, o: (s, 0))
-    block = (step_groups, rows, feat)
-    piece = pl.BlockSpec(block, lambda s, o: (s, 0, 0))
     return pl.pallas_call(
         functools.partial(expert_kernel, expert_count),
         grid_spec=pltpu.PrefetchScalarGridSpec(
             num_scalar_prefetch=1,
-            grid=(steps,),
+            grid=(groups // step_groups,),
             in_specs=[
                 straight,
                 straight,
-                piece,
-                piece,
-                piece,
-                pl.BlockSpec(block, lambda s, o: (jnp.minimum(s, steps // 2 - 1), 0, 0)),
-                pl.BlockSpec(block, lambda s, o: (jnp.maximum(s - steps // 2, 0), 0, 0)),
+                pl.BlockSpec((step_groups, pipes, rows, feat), lambda s, o: (s, 0, 0, 0)),
                 whole((width, hidden)),
                 whole((width, hidden)),
                 whole((hidden, width)),
             ],
             out_specs=[
-                flipped,
-                flipped,
-                flipped,
+                straight,
+                straight,
+                straight,
                 pl.BlockSpec((step_groups, pipes, rows, half), lambda s, o: (s, 0, 0, 0)),
                 pl.BlockSpec((expert_count, pipes, step_slots, half), lambda s, o: (0, 0, s, 0)),
             ],
         ),
-        out_shape=[jax.ShapeDtypeStruct((hidden, everything), BF16)] * 3
+        out_shape=[jax.ShapeDtypeStruct((everything, hidden), BF16)] * 3
         + [
             jax.ShapeDtypeStruct((groups, pipes, rows, half), BF16),
             jax.ShapeDtypeStruct((expert_count, pipes, everything // expert_count, half), BF16),
@@ -191,29 +193,30 @@
         compiler_params=pltpu.CompilerParams(vmem_limit_bytes=58 * MIB),
         name="expert",
         interpret=INTERPRET,
-    )(order, gate, up, *c, wg, wu, wd)
-
-
-def weight_kernel(order_ref, x_ref, c0_ref, c1_ref, c3_ref, c2x_ref, c2y_ref, act_ref, gg_ref, ug_ref, dwg_ref, dwu_ref, dwd_ref):
+    )(order, gate, up, x, wg, wu, wd)
+
+
+def weight_kernel(order_ref, x_ref, own_ref, before_ref, after_ref, early_ref, late_ref, act_ref, gg_ref, ug_ref, dwg_ref, dwu_ref, dwd_ref):
     groups, _, rows, feat = x_ref.shape
     step = pl.program_id(0)
-    features = x_ref[:, 0].reshape(groups * rows, feat)
-    dwg_ref[...] = dot(gg_ref[...], features).astype(BF16).T
-    dwu_ref[...] = dot(ug_ref[...], features).astype(BF16).T
-
-    def down(value):
-        dwd_ref[...] = dot(act_ref[...], value.reshape(groups * rows, feat)).astype(BF16)
-
-    pl.when(step == 0)(lambda: down(c0_ref[...]))
-    pl.when(step == 1)(lambda: down(c3_ref[...]))
-    pl.when(step == 2)(lambda: down(jnp.concatenate([c2x_ref[...], c2y_ref[...]], axis=0)))
-    pl.when(step == 3)(lambda: down(c1_ref[...]))
+    cotangent = x_ref[:, 0].reshape(groups * rows, feat)
+    dwd_ref[...] = dot(act_ref[...], cotangent, TN).astype(BF16)
+
+    def wide(value):
+        features = value.reshape(groups * rows, feat)
+        dwg_ref[...] = dot(gg_ref[...], features, TN).astype(BF16).T
+        dwu_ref[...] = dot(ug_ref[...], features, TN).astype(BF16).T
+
+    pl.when(step == 0)(lambda: wide(own_ref[...]))
+    pl.when(step == 1)(lambda: wide(after_ref[...]))
+    pl.when(step == 2)(lambda: wide(jnp.concatenate([early_ref[...], late_ref[...]], axis=0)))
+    pl.when(step == 3)(lambda: wide(before_ref[...]))
 
 
 def run_weights(order, x, c, act, gg, ug):
     groups, pipes, rows, feat = x.shape
-    hidden, everything = act.shape
-    whole = pl.BlockSpec((hidden, everything), lambda p, o: (0, 0))
+    everything, hidden = act.shape
+    whole = pl.BlockSpec((everything, hidden), lambda p, o: (0, 0))
     piece = lambda v: pl.BlockSpec(v.shape, lambda p, o: (0, 0, 0))
     return pl.pallas_call(
         weight_kernel,
@@ -314,6 +317,24 @@
     )(at, x, down1, down2, down3, up3, up2, up1, far_up, far_down)
 
 
+def stack_kernel(*refs):
+    for k, piece in enumerate(refs[:-1]):
+        refs[-1][k] = piece[...]
+
+
+def run_stack(pieces):
+    here = pl.BlockSpec(memory_space=pltpu.VMEM)
+    return pl.pallas_call(
+        stack_kernel,
+        in_specs=[here] * len(pieces),
+        out_specs=here,
+        out_shape=jax.ShapeDtypeStruct((len(pieces),) + pieces[0].shape, BF16),
+        compiler_params=pltpu.CompilerParams(vmem_limit_bytes=6 * MIB),
+        name="stack",
+        interpret=INTERPRET,
+    )(*pieces)
+
+
 def pipes_ring(x):
     cut = x.shape[0] // 2
     up1, down1 = shift(x, "pipe", 1), shift(x, "pipe", -1)
@@ -329,18 +350,19 @@
     capacity = max(token_count // 2, 2 * token_count // expert_count)
     slot_total = expert_count * capacity
     half = feat // 2
-    pieces = (tokens, shift(tokens, "pipe", -1), shift(tokens, "pipe", 2), shift(tokens, "pipe", 1))
     sent, slot_index, picker = run_dispatch(
-        expert_ids.T, gate_values.T, out_grad, pieces, expert_count, capacity
+        expert_ids.T, gate_values.T, out_grad, (tokens,), expert_count, capacity
     )
     received = lax.all_to_all(sent, "expert", split_axis=0, concat_axis=0, tiled=True)
-    near = received[:, :pipe_count].transpose(1, 0, 2, 3).reshape(1, pipe_count, slot_total, feat)
-    x = lax.all_gather(near, "dp", axis=0, tiled=True)
-    c = pipes_ring(groups_ring(received[:, pipe_count].reshape(slot_total, feat)))
+    c = pipes_ring(groups_ring(received[:, 0].reshape(slot_total, feat)))
+    own = received[:, 1].reshape(slot_total, feat)
+    near = (own, shift(own, "pipe", -1), shift(own, "pipe", 2), shift(own, "pipe", 1))
+    near = run_stack(near)
+    x = lax.all_gather(near[None], "dp", axis=0, tiled=True)
     order = (lax.axis_index("pipe") + jnp.arange(pipe_count, dtype=jnp.int32)) % pipe_count
-    gate, up = run_project(order, x, w_gate[0], w_up[0], group_count // 4)
+    gate, up = run_project(order, c, w_gate[0], w_up[0], group_count // 4)
     act, gg, ug, ring, cross = run_expert(
-        order, gate, up, c, w_gate[0], w_up[0], w_down[0], expert_count, group_count // 4
+        order, gate, up, x, w_gate[0], w_up[0], w_down[0], expert_count, group_count // 4
     )
     over_groups = lax.psum_scatter(
         ring.reshape(group_count, pipe_count * slot_total, half), "dp", scatter_dimension=0, tiled=True

time: 256 us -> 265 us (1.035)
  waiting for transfers between devices: 101 us -> 121 us
  blocking collectives: 47.9 us -> 40.6 us
  local copies, waits for them, and re-layouts: 5.52 us -> 1.58 us
    ppermute x15, waiting for transfers between devices: 59.1 us -> 82.3 us  [shift(): return lax.ppermute(x, axis, [(k, (k + by) % count) for k in range(count)])]
    all_to_all x1, blocking collectives: 20.5 us -> 14.6 us  [body(): lax.all_to_all(sent, 'expert', split_axis=0, concat_axis=0, tiled=True)]
    all_gather x1, waiting for transfers between devices: 4.96 us -> 0.01 us  [body(): x = lax.all_gather(near[None], 'dp', axis=0, tiled=True)]
    ppermute x15, starting transfers between devices: 25.8 us -> 22.5 us  [shift(): return lax.ppermute(x, axis, [(k, (k + by) % count) for k in range(count)])]
    unnamed x16 -> x12, local copies, waits for them, and re-layouts: 4.38 us -> 1.43 us
  transfers between devices with their start and end apart: 21 -> 21, of which waited for: 16 -> 14; matrix products, arithmetic and copies ran while one was open for 1% -> 1% of each run, Pallas kernels for 9% -> 9%
where the time goes in v1:
time: 265 us; the launch traced here: 264 us
  waiting for transfers between devices  121 us (46%)
  starting transfers between devices  45.3 us (17%)
  blocking collectives  40.6 us (15%)
  Pallas kernels  39.8 us (15%)
  between operations  13.9 us (5%)
    ppermute x15, waiting for transfers between devices, shift(): return lax.ppermute(x, axis, [(k, (k + by) % count) for k in range(count)])  82.3 us
    ppermute x15, starting transfers between devices, shift(): return lax.ppermute(x, axis, [(k, (k + by) % count) for k in range(count)])  22.5 us
    all_to_all x1, blocking collectives, body(): lax.all_to_all(sent, 'expert', split_axis=0, concat_axis=0, tiled=True)  14.6 us
    pallas_call x1, Pallas kernels, run_expert(): pl.pallas_call(functools.partial(expert_kernel, expert_count), grid_spec=...  14.3 us
    all_gather x1, blocking collectives, body(): column_slots = lax.all_gather(late_index[None], 'dp', axis=0, tiled=True)  13.7 us
    reduce_scatter x1, waiting for transfers between devices, body(): lax.psum_scatter(over_groups.reshape(pipe_count, slot_total, half), 'pipe...  13.2 us
    pallas_call x1, Pallas kernels, run_weights(): pl.pallas_call(weight_kernel, grid_spec=pltpu.PrefetchScalarGridSpec(num_...  12.5 us
    all_to_all x1, blocking collectives, body(): lax.all_to_all(column, 'pipe', split_axis=0, concat_axis=0, tiled=True)  12.3 us
  transfers between devices with their start and end apart: 21, of which 14 were waited for; matrix products, arithmetic and copies ran while one was open for 1% of the time, Pallas kernels for 9%

profile of v1, /device:TPU:1, one launch (start us, length us, event | category | flops | bytes accessed | tf_op | source)
XLA Modules:
  0.0 264.0 jit_solution(9167711726103000922)
XLA Ops:
  7.2 2.0 dispatch.1
  9.2 14.6 %all_to_all.25 = bf16[8,2,16,768]{3,2,1,0:T(8,128)(2,1)S(1)} all-to-all(bf16[8,2,16,768]{3,2,1,0:T(8,128)(2,1)} %get-tuple-element.23), channel_id=1, replica_groups=mesh['expert'=8,'dp'=8,'pipe'=4] {'expert'}, dimensions={0} | all-to-all | bytes 786432 | tf_op jit(solution)/shard_map/all_to_all | solution.py:356
  23.8 2.0 collective-permute-start.12
  26.9 2.6 collective-permute-done.12.refs_1_
  29.5 3.2 %collective-permute-done.13.refs_2_ = bf16[128,768]{1,0:T(8,128)(2,1)S(1)} collective-permute-done((bf16[128,768]{1,0:T(8,128)(2,1)S(1)}, bf16[128,768]{1,0:T(8,128)(2,1)S(1)}, u32[]{:S(2)}, u32[]{:S(2)}) %collective-permute-start.13) | collective-permute-done | bytes 196640 | tf_op jit(solution)/shard_map/ppermute | solution.py:286
  32.7 5.7 %collective-permute-done.14.refs_3_ = bf16[128,768]{1,0:T(8,128)(2,1)S(1)} collective-permute-done((bf16[128,768]{1,0:T(8,128)(2,1)S(1)}, bf16[128,768]{1,0:T(8,128)(2,1)S(1)}, u32[]{:S(2)}, u32[]{:S(2)}) %collective-permute-start.14) | collective-permute-done | bytes 196640 | tf_op jit(solution)/shard_map/ppermute | solution.py:286
  39.4 1.7 collective-permute-start.3
  41.1 4.0 %collective-permute-start = (bf16[128,768]{1,0:T(8,128)(2,1)S(1)}, bf16[128,768]{1,0:T(8,128)(2,1)S(1)}, u32[]{:S(2)}, u32[]{:S(2)}) collective-permute-start(bf16[128,768]{1,0:T(8,128)(2,1)S(1)} %bitcast.26), channel_id=1, source_target_pairs={{0,28},{4,0},{8,4},{12,8},{16,12},{20,16},{24,20},{28,24},{1,29},{... | collective-permute-start | bytes 589832 | tf_op jit(solution)/shard_map/ppermute | solution.py:286
  45.1 4.7 %collective-permute-done.3.refs_6_ = bf16[128,768]{1,0:T(8,128)(2,1)S(1)} collective-permute-done((bf16[128,768]{1,0:T(8,128)(2,1)S(1)}, bf16[128,768]{1,0:T(8,128)(2,1)S(1)}, u32[]{:S(2)}, u32[]{:S(2)}) %collective-permute-start.3) | collective-permute-done | bytes 196640 | tf_op jit(solution)/shard_map/ppermute | solution.py:286
  49.8 2.7 %collective-permute-start.1 = (bf16[128,768]{1,0:T(8,128)(2,1)S(1)}, bf16[128,768]{1,0:T(8,128)(2,1)S(1)}, u32[]{:S(2)}, u32[]{:S(2)}) collective-permute-start(bf16[128,768]{1,0:T(8,128)(2,1)S(1)} %collective-permute-done.refs_1_), channel_id=1, source_target_pairs={{0,28},{4,0},{8,4},{12,8},{16,12},{20,16},{24,20},{28,24},{1,29},{... | collective-permute-start | bytes 589832 | tf_op jit(solution)/shard_map/ppermute | solution.py:286
  52.5 9.0 %collective-permute-done.4.refs_5_ = bf16[128,768]{1,0:T(8,128)(2,1)S(1)} collective-permute-done((bf16[128,768]{1,0:T(8,128)(2,1)S(1)}, bf16[128,768]{1,0:T(8,128)(2,1)S(1)}, u32[]{:S(2)}, u32[]{:S(2)}) %collective-permute-start.4) | collective-permute-done | bytes 196640 | tf_op jit(solution)/shard_map/ppermute | solution.py:286
  61.5 2.7 %collective-permute-start.2 = (bf16[128,768]{1,0:T(8,128)(2,1)S(1)}, bf16[128,768]{1,0:T(8,128)(2,1)S(1)}, u32[]{:S(2)}, u32[]{:S(2)}) collective-permute-start(bf16[128,768]{1,0:T(8,128)(2,1)S(1)} %collective-permute-done.1.refs_2_), channel_id=1, source_target_pairs={{0,28},{4,0},{8,4},{12,8},{16,12},{20,16},{24,20},{28,24},{1,29},{... | collective-permute-start | bytes 589832 | tf_op jit(solution)/shard_map/ppermute | solution.py:286
  64.2 9.1 %collective-permute-done.5.refs_4_ = bf16[128,768]{1,0:T(8,128)(2,1)S(1)} collective-permute-done((bf16[128,768]{1,0:T(8,128)(2,1)S(1)}, bf16[128,768]{1,0:T(8,128)(2,1)S(1)}, u32[]{:S(2)}, u32[]{:S(2)}) %collective-permute-start.5) | collective-permute-done | bytes 196640 | tf_op jit(solution)/shard_map/ppermute | solution.py:286
  73.4 2.7 %collective-permute-start.7 = (bf16[64,768]{1,0:T(8,128)(2,1)S(1)}, bf16[64,768]{1,0:T(8,128)(2,1)S(1)}, u32[]{:S(2)}, u32[]{:S(2)}) collective-permute-start(bf16[64,768]{1,0:T(8,128)(2,1)S(1)} %slice.74), channel_id=1, source_target_pairs={{0,28},{4,0},{8,4},{12,8},{16,12},{20,16},{24,20},{28,24},{1,29},{... | collective-permute-start | bytes 294920 | tf_op jit(solution)/shard_map/ppermute | solution.py:286
  76.2 4.6 %collective-permute-done.6.refs_7_ = bf16[64,768]{1,0:T(8,128)(2,1)S(1)} collective-permute-done((bf16[64,768]{1,0:T(8,128)(2,1)S(1)}, bf16[64,768]{1,0:T(8,128)(2,1)S(1)}, u32[]{:S(2)}, u32[]{:S(2)}) %collective-permute-start.6) | collective-permute-done | bytes 98336 | tf_op jit(solution)/shard_map/ppermute | solution.py:286
  81.5 2.7 %collective-permute-start.9 = (bf16[8,128,768]{2,1,0:T(8,128)(2,1)S(1)}, bf16[8,128,768]{2,1,0:T(8,128)(2,1)S(1)}, u32[]{:S(2)}, u32[]{:S(2)}) collective-permute-start(bf16[8,128,768]{2,1,0:T(8,128)(2,1)S(1)} %place.1.refs_0_.own_ref), channel_id=1, source_target_pairs={{0,3},{1,0},{2,1},{3,2},{4,7},{5,4},{6,5},{7,6},{8,11},{9,8},{10,9... | collective-permute-start | bytes 4718600 | tf_op jit(solution)/shard_map/ppermute | solution.py:286
  84.2 31.3 %collective-permute-done.8.refs_1_.before_ref = bf16[8,128,768]{2,1,0:T(8,128)(2,1)S(1)} collective-permute-done((bf16[8,128,768]{2,1,0:T(8,128)(2,1)S(1)}, bf16[8,128,768]{2,1,0:T(8,128)(2,1)S(1)}, u32[]{:S(2)}, u32[]{:S(2)}) %collective-permute-start.8) | collective-permute-done | bytes 1572896 | tf_op jit(solution)/shard_map/ppermute | solution.py:286
  115.7 1.2 copy-done.2
  117.2 2.6 collective-permute-start.11
  120.4 11.7 %collective-permute-done.10.refs_3_.early_ref = bf16[4,128,768]{2,1,0:T(8,128)(2,1)} collective-permute-done((bf16[4,128,768]{2,1,0:T(8,128)(2,1)S(1)}, bf16[4,128,768]{2,1,0:T(8,128)(2,1)}, u32[]{:S(2)}, u32[]{:S(2)}) %collective-permute-start.10) | collective-permute-done | bytes 786464 | tf_op jit(solution)/shard_map/ppermute | solution.py:286
  132.4 8.8 %project.1 = (f32[1024,256]{1,0:T(8,128)}, f32[1024,256]{1,0:T(8,128)}) custom-call(s32[4]{0:T(128)} %and_select_fusion.1.order_ref, bf16[8,128,768]{2,1,0:T(8,128)(2,1)} %copy-done, bf16[8,128,768]{2,1,0:T(8,128)(2,1)} %copy-done.1, bf16[8,128,768]{2,1,0:T(8,128)(2,1)} %copy-done.2, bf16[4,128,768]{2,1,0:T(8,128)(2,1)} %collective-permute-done.10.refs_3_.early_ref, ...), custom_call_target="tpu_custom_call" | custom-call | tf_op jit(solution)/shard_map/project/pallas_call | solution.py:105
  141.3 14.3 %expert.1 = (bf16[1024,256]{1,0:T(8,128)(2,1)}, bf16[1024,256]{1,0:T(8,128)(2,1)}, bf16[1024,256]{1,0:T(8,128)(2,1)}, bf16[8,4,128,384]{3,2,1,0:T(8,128)(2,1)}, bf16[8,4,128,384]{3,2,1,0:T(8,128)(2,1)}) custom-call(s32[4]{0:T(128)} %and_select_fusion.1.order_ref, f32[1024,256]{1,0:T(8,128)} %get-tuple-element.24.gate_ref, ...), custom_call_target="tpu_custom_call" | custom-call | tf_op jit(solution)/shard_map/expert/pallas_call | solution.py:167
  155.6 8.7 %all-to-all-start.2 = ((bf16[8,4,128,384]{3,2,1,0:T(8,128)(2,1)}), bf16[8,4,128,384]{3,2,1,0:T(8,128)(2,1)S(1)}, u32[]{:S(2)}, u32[]{:S(2)}) async-start(bf16[8,4,128,384]{3,2,1,0:T(8,128)(2,1)} %get-tuple-element.35), calls=%async_computation.4 | async-start | bytes 6291456 | tf_op jit(solution)/shard_map/all_to_all | solution.py:370
  164.3 12.5 %weights.1 = (bf16[3072,256]{1,0:T(8,128)(2,1)}, bf16[3072,256]{1,0:T(8,128)(2,1)}, bf16[256,3072]{1,0:T(8,128)(2,1)}) custom-call(s32[4]{0:T(128)} %and_select_fusion.1.order_ref, bf16[8,4,128,768]{3,2,1,0:T(8,128)(2,1)} %bitcast.29, bf16[8,128,768]{2,1,0:T(8,128)(2,1)} %copy-done, bf16[8,128,768]{2,1,0:T(8,128)(2,1)} %copy-done.1, ...), custom_call_target="tpu_custom_call" | custom-call | tf_op jit(solution)/shard_map/weights/pallas_call | solution.py:221
  176.8 13.7 %all-gather.2.slots_ref = s32[8,2,32]{2,1,0:T(2,128)S(1)} all-gather(s32[1,2,32]{2,1,0:T(2,128)S(1)} %bitcast.41), channel_id=3, replica_groups=mesh['expert'=8,'dp'=8,'pipe'=4] {'dp'}, dimensions={0}, use_global_device_ids=true | all-gather | bytes 2304 | tf_op jit(solution)/shard_map/all_gather | solution.py:372
  190.4 12.0 %reduce-scatter.3.cloned.1.call-done = bf16[1,512,384]{2,1,0:T(8,128)(2,1)} async-done(((bf16[8,512,384]{2,1,0:T(8,128)(2,1)}), bf16[1,512,384]{2,1,0:T(8,128)(2,1)}) %reduce-scatter.3.cloned.1.call-update) | async-done | bytes 393232 | tf_op jit(solution)/shard_map/reduce_scatter | solution.py:367
  203.2 12.3 %all_to_all.26 = bf16[4,256,384]{2,1,0:T(8,128)(2,1)S(1)} all-to-all(bf16[4,256,384]{2,1,0:T(8,128)(2,1)S(1)} %combine.1), channel_id=1, replica_groups=mesh['expert'=8,'dp'=8,'pipe'=4] {'pipe'}, dimensions={0} | all-to-all | bytes 1572864 | tf_op jit(solution)/shard_map/all_to_all | solution.py:381
  215.5 13.2 %reduce-scatter.5.cloned.1.call-done = bf16[1,128,384]{2,1,0:T(8,128)(2,1)} async-done(((bf16[4,128,384]{2,1,0:T(8,128)(2,1)}), bf16[1,128,384]{2,1,0:T(8,128)(2,1)}) %reduce-scatter.5.cloned.1.call-update) | async-done | bytes 98320 | tf_op jit(solution)/shard_map/reduce_scatter | solution.py:377
  228.8 7.3 %all-to-all-start.1 = ((bf16[8,16,384]{2,1,0:T(8,128)(2,1)}), bf16[8,16,384]{2,1,0:T(8,128)(2,1)S(1)}, u32[]{:S(2)}, u32[]{:S(2)}) async-start(bf16[8,16,384]{2,1,0:T(8,128)(2,1)} %bitcast.38), calls=%async_computation.3 | async-start | bytes 196608 | tf_op jit(solution)/shard_map/all_to_all | solution.py:391
  236.9 4.2 %all-to-all-done.1 = bf16[8,16,384]{2,1,0:T(8,128)(2,1)S(1)} async-done(((bf16[8,16,384]{2,1,0:T(8,128)(2,1)}), bf16[8,16,384]{2,1,0:T(8,128)(2,1)S(1)}, u32[]{:S(2)}, u32[]{:S(2)}) %all-to-all-start.1) | async-done | bytes 98336 | tf_op jit(solution)/shard_map/all_to_all | solution.py:391
  241.1 6.8 %all-to-all-start.4 = ((bf16[8,32,384]{2,1,0:T(8,128)(2,1)}), bf16[8,32,384]{2,1,0:T(8,128)(2,1)S(1)}, u32[]{:S(2)}, u32[]{:S(2)}) async-start(bf16[8,32,384]{2,1,0:T(8,128)(2,1)} %bitcast.13), calls=%async_computation.6 | async-start | bytes 393216 | tf_op jit(solution)/shard_map/all_to_all | solution.py:383
  248.0 8.8 %all-to-all-done.4 = bf16[8,32,384]{2,1,0:T(8,128)(2,1)S(1)} async-done(((bf16[8,32,384]{2,1,0:T(8,128)(2,1)}), bf16[8,32,384]{2,1,0:T(8,128)(2,1)S(1)}, u32[]{:S(2)}, u32[]{:S(2)}) %all-to-all-start.4) | async-done | bytes 196640 | tf_op jit(solution)/shard_map/all_to_all | solution.py:383
  (46 shorter events, 6.6 us)
Async XLA Ops:
  7.2 134.1 %all-gather.5.cloned.1.call-start = ((), (), s32[]{:S(2)}) async-start(), calls=%async_computation.9 | async-start | bytes 7077888 | tf_op jit(solution)/shard_map/all_gather | solution.py:361
  23.8 52.4 %copy-start.5 = (s32[8]{0:T(128)S(1)}, s32[8]{0:T(128)}, u32[]{:S(2)}) copy-start(s32[8]{0:T(128)} %constant.40.clone) | copy-start | bytes 100
  23.8 5.7 %collective-permute-start.12 = (bf16[128,768]{1,0:T(8,128)(2,1)S(1)}, bf16[128,768]{1,0:T(8,128)(2,1)S(1)}, u32[]{:S(2)}, u32[]{:S(2)}) collective-permute-start(bf16[128,768]{1,0:T(8,128)(2,1)S(1)} %bitcast.21), channel_id=1, source_target_pairs={{0,3},{1,0},{2,1},{3,2},{4,7},{5,4},{6,5},{7,6},{8,11},{9,8},{10,9... | collective-permute-start | bytes 589832 | tf_op jit(solution)/shard_map/ppermute | solution.py:286
  25.9 6.9 %collective-permute-start.13 = (bf16[128,768]{1,0:T(8,128)(2,1)S(1)}, bf16[128,768]{1,0:T(8,128)(2,1)S(1)}, u32[]{:S(2)}, u32[]{:S(2)}) collective-permute-start(bf16[128,768]{1,0:T(8,128)(2,1)S(1)} %bitcast.22), channel_id=1, source_target_pairs={{0,2},{1,3},{2,0},{3,1},{4,6},{5,7},{6,4},{7,5},{8,10},{9,11},{10,... | collective-permute-start | bytes 589832 | tf_op jit(solution)/shard_map/ppermute | solution.py:286
  26.2 12.2 %collective-permute-start.14 = (bf16[128,768]{1,0:T(8,128)(2,1)S(1)}, bf16[128,768]{1,0:T(8,128)(2,1)S(1)}, u32[]{:S(2)}, u32[]{:S(2)}) collective-permute-start(bf16[128,768]{1,0:T(8,128)(2,1)S(1)} %bitcast.23), channel_id=1, source_target_pairs={{0,1},{1,2},{2,3},{3,0},{4,5},{5,6},{6,7},{7,4},{8,9},{9,10},{10,1... | collective-permute-start | bytes 589832 | tf_op jit(solution)/shard_map/ppermute | solution.py:286
  39.4 163.1 %reduce-scatter.3.cloned.1.call-start = ((), (), s32[]{:S(2)}) async-start(), calls=%async_computation.7 | async-start | bytes 3538944 | tf_op jit(solution)/shard_map/reduce_scatter | solution.py:367
  39.4 10.4 %collective-permute-start.3 = (bf16[128,768]{1,0:T(8,128)(2,1)S(1)}, bf16[128,768]{1,0:T(8,128)(2,1)S(1)}, u32[]{:S(2)}, u32[]{:S(2)}) collective-permute-start(bf16[128,768]{1,0:T(8,128)(2,1)S(1)} %bitcast.25), channel_id=1, source_target_pairs={{0,4},{4,8},{8,12},{12,16},{16,20},{20,24},{24,28},{28,0},{1,5},{5... | collective-permute-start | bytes 589832 | tf_op jit(solution)/shard_map/ppermute | solution.py:286
  41.1 8.7 %collective-permute-start = (bf16[128,768]{1,0:T(8,128)(2,1)S(1)}, bf16[128,768]{1,0:T(8,128)(2,1)S(1)}, u32[]{:S(2)}, u32[]{:S(2)}) collective-permute-start(bf16[128,768]{1,0:T(8,128)(2,1)S(1)} %bitcast.26), channel_id=1, source_target_pairs={{0,28},{4,0},{8,4},{12,8},{16,12},{20,16},{24,20},{28,24},{1,29},{... | collective-permute-start | bytes 589832 | tf_op jit(solution)/shard_map/ppermute | solution.py:286
  49.8 11.7 %collective-permute-start.4 = (bf16[128,768]{1,0:T(8,128)(2,1)S(1)}, bf16[128,768]{1,0:T(8,128)(2,1)S(1)}, u32[]{:S(2)}, u32[]{:S(2)}) collective-permute-start(bf16[128,768]{1,0:T(8,128)(2,1)S(1)} %collective-permute-done.3.refs_6_), channel_id=1, source_target_pairs={{0,4},{4,8},{8,12},{12,16},{16,20},{20,24},{24,28},{28,0},{1,5},{5... | collective-permute-start | bytes 589832 | tf_op jit(solution)/shard_map/ppermute | solution.py:286
  49.8 11.7 %collective-permute-start.1 = (bf16[128,768]{1,0:T(8,128)(2,1)S(1)}, bf16[128,768]{1,0:T(8,128)(2,1)S(1)}, u32[]{:S(2)}, u32[]{:S(2)}) collective-permute-start(bf16[128,768]{1,0:T(8,128)(2,1)S(1)} %collective-permute-done.refs_1_), channel_id=1, source_target_pairs={{0,28},{4,0},{8,4},{12,8},{16,12},{20,16},{24,20},{28,24},{1,29},{... | collective-permute-start | bytes 589832 | tf_op jit(solution)/shard_map/ppermute | solution.py:286
  61.5 11.8 %collective-permute-start.5 = (bf16[128,768]{1,0:T(8,128)(2,1)S(1)}, bf16[128,768]{1,0:T(8,128)(2,1)S(1)}, u32[]{:S(2)}, u32[]{:S(2)}) collective-permute-start(bf16[128,768]{1,0:T(8,128)(2,1)S(1)} %collective-permute-done.4.refs_5_), channel_id=1, source_target_pairs={{0,4},{4,8},{8,12},{12,16},{16,20},{20,24},{24,28},{28,0},{1,5},{5... | collective-permute-start | bytes 589832 | tf_op jit(solution)/shard_map/ppermute | solution.py:286
  61.5 11.9 %collective-permute-start.2 = (bf16[128,768]{1,0:T(8,128)(2,1)S(1)}, bf16[128,768]{1,0:T(8,128)(2,1)S(1)}, u32[]{:S(2)}, u32[]{:S(2)}) collective-permute-start(bf16[128,768]{1,0:T(8,128)(2,1)S(1)} %collective-permute-done.1.refs_2_), channel_id=1, source_target_pairs={{0,28},{4,0},{8,4},{12,8},{16,12},{20,16},{24,20},{28,24},{1,29},{... | collective-permute-start | bytes 589832 | tf_op jit(solution)/shard_map/ppermute | solution.py:286
  73.3 7.4 %collective-permute-start.6 = (bf16[64,768]{1,0:T(8,128)(2,1)S(1)}, bf16[64,768]{1,0:T(8,128)(2,1)S(1)}, u32[]{:S(2)}, u32[]{:S(2)}) collective-permute-start(bf16[64,768]{1,0:T(8,128)(2,1)S(1)} %slice.73), channel_id=1, source_target_pairs={{0,4},{4,8},{8,12},{12,16},{16,20},{20,24},{24,28},{28,0},{1,5},{5... | collective-permute-start | bytes 294920 | tf_op jit(solution)/shard_map/ppermute | solution.py:286
  73.4 7.3 %collective-permute-start.7 = (bf16[64,768]{1,0:T(8,128)(2,1)S(1)}, bf16[64,768]{1,0:T(8,128)(2,1)S(1)}, u32[]{:S(2)}, u32[]{:S(2)}) collective-permute-start(bf16[64,768]{1,0:T(8,128)(2,1)S(1)} %slice.74), channel_id=1, source_target_pairs={{0,28},{4,0},{8,4},{12,8},{16,12},{20,16},{24,20},{28,24},{1,29},{... | collective-permute-start | bytes 294920 | tf_op jit(solution)/shard_map/ppermute | solution.py:286
  81.4 35.6 %copy-start = (bf16[8,128,768]{2,1,0:T(8,128)(2,1)}, bf16[8,128,768]{2,1,0:T(8,128)(2,1)S(1)}, u32[]{:S(2)}) copy-start(bf16[8,128,768]{2,1,0:T(8,128)(2,1)S(1)} %place.1.refs_0_.own_ref) | copy-start | bytes 4718596
  81.4 34.1 %collective-permute-start.8 = (bf16[8,128,768]{2,1,0:T(8,128)(2,1)S(1)}, bf16[8,128,768]{2,1,0:T(8,128)(2,1)S(1)}, u32[]{:S(2)}, u32[]{:S(2)}) collective-permute-start(bf16[8,128,768]{2,1,0:T(8,128)(2,1)S(1)} %place.1.refs_0_.own_ref), channel_id=1, source_target_pairs={{0,1},{1,2},{2,3},{3,0},{4,5},{5,6},{6,7},{7,4},{8,9},{9,10},{10,1... | collective-permute-start | bytes 4718600 | tf_op jit(solution)/shard_map/ppermute | solution.py:286
  81.5 34.1 %collective-permute-start.9 = (bf16[8,128,768]{2,1,0:T(8,128)(2,1)S(1)}, bf16[8,128,768]{2,1,0:T(8,128)(2,1)S(1)}, u32[]{:S(2)}, u32[]{:S(2)}) collective-permute-start(bf16[8,128,768]{2,1,0:T(8,128)(2,1)S(1)} %place.1.refs_0_.own_ref), channel_id=1, source_target_pairs={{0,3},{1,0},{2,1},{3,2},{4,7},{5,4},{6,5},{7,6},{8,11},{9,8},{10,9... | collective-permute-start | bytes 4718600 | tf_op jit(solution)/shard_map/ppermute | solution.py:286
  115.5 1.6 copy-start.1
  115.6 16.5 %collective-permute-start.10 = (bf16[4,128,768]{2,1,0:T(8,128)(2,1)S(1)}, bf16[4,128,768]{2,1,0:T(8,128)(2,1)}, u32[]{:S(2)}, u32[]{:S(2)}) collective-permute-start(bf16[4,128,768]{2,1,0:T(8,128)(2,1)S(1)} %slice.75), channel_id=1, source_target_pairs={{0,1},{1,2},{2,3},{3,0},{4,5},{5,6},{6,7},{7,4},{8,9},{9,10},{10,1... | collective-permute-start | bytes 2359304 | tf_op jit(solution)/shard_map/ppermute | solution.py:286
  115.7 1.3 copy-start.2
  117.2 15.3 %collective-permute-start.11 = (bf16[4,128,768]{2,1,0:T(8,128)(2,1)S(1)}, bf16[4,128,768]{2,1,0:T(8,128)(2,1)}, u32[]{:S(2)}, u32[]{:S(2)}) collective-permute-start(bf16[4,128,768]{2,1,0:T(8,128)(2,1)S(1)} %slice.76), channel_id=1, source_target_pairs={{0,3},{1,0},{2,1},{3,2},{4,7},{5,4},{6,5},{7,6},{8,11},{9,8},{10,9... | collective-permute-start | bytes 2359304 | tf_op jit(solution)/shard_map/ppermute | solution.py:286
  155.6 46.9 %all-to-all-start.2 = ((bf16[8,4,128,384]{3,2,1,0:T(8,128)(2,1)}), bf16[8,4,128,384]{3,2,1,0:T(8,128)(2,1)S(1)}, u32[]{:S(2)}, u32[]{:S(2)}) async-start(bf16[8,4,128,384]{3,2,1,0:T(8,128)(2,1)} %get-tuple-element.35), calls=%async_computation.4 | async-start | bytes 6291456 | tf_op jit(solution)/shard_map/all_to_all | solution.py:370
  164.3 64.5 %reduce-scatter.5.cloned.1.call-start = ((), (), s32[]{:S(2)}) async-start(), calls=%async_computation.8 | async-start | bytes 491520 | tf_op jit(solution)/shard_map/reduce_scatter | solution.py:377
  164.3 12.5 %copy-start.4 = (s32[2,32]{1,0:T(2,128)S(1)}, s32[2,32]{1,0:T(2,128)}, u32[]{:S(2)}) copy-start(s32[2,32]{1,0:T(2,128)} %get-tuple-element.29) | copy-start | bytes 772
  203.2 44.6 %copy-start.3 = (bf16[128,32]{1,0:T(8,128)(2,1)S(1)}, bf16[128,32]{1,0:T(8,128)(2,1)}, u32[]{:S(2)}) copy-start(bf16[128,32]{1,0:T(8,128)(2,1)} %get-tuple-element.22) | copy-start | bytes 24580
  228.8 12.3 %all-to-all-start.1 = ((bf16[8,16,384]{2,1,0:T(8,128)(2,1)}), bf16[8,16,384]{2,1,0:T(8,128)(2,1)S(1)}, u32[]{:S(2)}, u32[]{:S(2)}) async-start(bf16[8,16,384]{2,1,0:T(8,128)(2,1)} %bitcast.38), calls=%async_computation.3 | async-start | bytes 196608 | tf_op jit(solution)/shard_map/all_to_all | solution.py:391
  241.1 15.7 %all-to-all-start.4 = ((bf16[8,32,384]{2,1,0:T(8,128)(2,1)}), bf16[8,32,384]{2,1,0:T(8,128)(2,1)S(1)}, u32[]{:S(2)}, u32[]{:S(2)}) async-start(bf16[8,32,384]{2,1,0:T(8,128)(2,1)} %bitcast.13), calls=%async_computation.6 | async-start | bytes 393216 | tf_op jit(solution)/shard_map/all_to_all | solution.py:383
Sparse Core Ops, SparseCore 0:
  39.5 83.1 all-gather.4
  155.7 46.7 reduce-scatter.2
  205.0 23.7 reduce-scatter.4

commit v2 on v1

--- a/solution.py
+++ b/solution.py
@@ -72,18 +72,12 @@
     )(ids, gates, out_grad, *pieces)
 
 
-def in_order(pieces, early):
-    own, before, after, far_early, far_late = pieces
-    return own[...], after[...], jnp.where(early, far_early[...], far_late[...]), before[...]
-
-
 def project_kernel(order_ref, *refs):
-    pieces, (wg_ref, wu_ref, gate_ref, up_ref) = refs[:5], refs[5:]
+    pieces, (wg_ref, wu_ref, gate_ref, up_ref) = refs[:3], refs[3:]
     groups, rows, feat = pieces[0].shape
-    early = pl.program_id(0) < pl.num_programs(0) // 2
     gate = up = None
-    for k, value in enumerate(in_order(pieces, early)):
-        features = value.reshape(groups * rows, feat)
+    for k, piece in zip((0, 3, 1), pieces):
+        features = piece[...].reshape(groups * rows, feat)
         cols = pl.ds(pl.multiple_of(order_ref[k] * feat, 128), feat)
         g = dot(features, wg_ref[cols, :])
         u = dot(features, wu_ref[cols, :])
@@ -96,26 +90,16 @@
 def run_project(order, c, wg, wu, step_groups):
     groups, rows, feat = c[0].shape
     width, hidden = wg.shape
-    steps = groups // step_groups
     step_rows = step_groups * rows
-    block = (step_groups, rows, feat)
-    piece = pl.BlockSpec(block, lambda s, o: (s, 0, 0))
+    piece = pl.BlockSpec((step_groups, rows, feat), lambda s, o: (s, 0, 0))
     whole = pl.BlockSpec((width, hidden), lambda s, o: (0, 0))
     result = pl.BlockSpec((step_rows, hidden), lambda s, o: (s, 0))
     return pl.pallas_call(
         project_kernel,
         grid_spec=pltpu.PrefetchScalarGridSpec(
             num_scalar_prefetch=1,
-            grid=(steps,),
-            in_specs=[
-                piece,
-                piece,
-                piece,
-                pl.BlockSpec(block, lambda s, o: (jnp.minimum(s, steps // 2 - 1), 0, 0)),
-                pl.BlockSpec(block, lambda s, o: (jnp.maximum(s - steps // 2, 0), 0, 0)),
-                whole,
-                whole,
-            ],
+            grid=(groups // step_groups,),
+            in_specs=[piece, piece, piece, whole, whole],
             out_specs=[result, result],
         ),
         out_shape=[jax.ShapeDtypeStruct((groups * rows, hidden), F32)] * 2,
@@ -125,7 +109,54 @@
     )(order, *c, wg, wu)
 
 
-def expert_kernel(expert_count, order_ref, gate_ref, up_ref, x_ref, wg_ref, wu_ref, wd_ref, act_ref, gg_ref, ug_ref, ring_ref, cross_ref):
+def activate_kernel(order_ref, gate_ref, up_ref, early_ref, late_ref, wg_ref, wu_ref, act_ref, slope_ref, linear_ref):
+    groups, rows, feat = early_ref.shape
+    early = pl.program_id(0) < pl.num_programs(0) // 2
+    features = jnp.where(early, early_ref[...], late_ref[...]).reshape(groups * rows, feat)
+    gate = gate_ref[...] + dot(features, wg_ref[...])
+    up = up_ref[...] + dot(features, wu_ref[...])
+    sig = jax.nn.sigmoid(gate)
+    linear = gate * sig
+    act_ref[...] = (linear * up).astype(BF16)
+    slope_ref[...] = up * (sig * (1.0 + gate * (1.0 - sig)))
+    linear_ref[...] = linear
+
+
+def run_activate(order, gate, up, far, wg, wu, step_groups):
+    everything, hidden = gate.shape
+    rows, feat = far[0].shape[1:]
+    step_rows = step_groups * rows
+    steps = everything // step_rows
+    block = (step_groups, rows, feat)
+    straight = pl.BlockSpec((step_rows, hidden), lambda s, o: (s, 0))
+    weight = pl.BlockSpec((feat, hidden), lambda s, o: (o[2], 0))
+    return pl.pallas_call(
+        activate_kernel,
+        grid_spec=pltpu.PrefetchScalarGridSpec(
+            num_scalar_prefetch=1,
+            grid=(steps,),
+            in_specs=[
+                straight,
+                straight,
+                pl.BlockSpec(block, lambda s, o: (jnp.minimum(s, steps // 2 - 1), 0, 0)),
+                pl.BlockSpec(block, lambda s, o: (jnp.maximum(s - steps // 2, 0), 0, 0)),
+                weight,
+                weight,
+            ],
+            out_specs=[straight, straight, straight],
+        ),
+        out_shape=[
+            jax.ShapeDtypeStruct((everything, hidden), BF16),
+            jax.ShapeDtypeStruct((everything, hidden), F32),
+            jax.ShapeDtypeStruct((everything, hidden), F32),
+        ],
+        compiler_params=pltpu.CompilerParams(vmem_limit_bytes=58 * MIB),
+        name="activate",
+        interpret=INTERPRET,
+    )(order, gate, up, *far, wg, wu)
+
+
+def expert_kernel(expert_count, order_ref, slope_ref, linear_ref, x_ref, wg_ref, wu_ref, wd_ref, gg_ref, ug_ref, ring_ref, cross_ref):
     groups, pipes, rows, feat = x_ref.shape
     total = groups * rows
     half = feat // 2
@@ -135,13 +166,8 @@
         cols = pl.ds(pl.multiple_of(order_ref[k] * feat, 128), feat)
         a = dot(x_ref[:, k].reshape(total, feat), wd_ref[:, cols], NT)
         act_grad = a if act_grad is None else act_grad + a
-    gate = gate_ref[...]
-    up = up_ref[...]
-    sig = jax.nn.sigmoid(gate)
-    linear = gate * sig
-    gate_grad = (act_grad * up * (sig * (1.0 + gate * (1.0 - sig)))).astype(BF16)
-    up_grad = (act_grad * linear).astype(BF16)
-    act_ref[...] = (linear * up).astype(BF16)
+    gate_grad = (act_grad * slope_ref[...]).astype(BF16)
+    up_grad = (act_grad * linear_ref[...]).astype(BF16)
     gg_ref[...] = gate_grad
     ug_ref[...] = up_grad
     for p in range(pipes):
@@ -155,7 +181,7 @@
             )
 
 
-def run_expert(order, gate, up, x, wg, wu, wd, expert_count, step_groups):
+def run_expert(order, slope, linear, x, wg, wu, wd, expert_count, step_groups):
     groups, pipes, rows, feat = x.shape
     width, hidden = wg.shape
     half = feat // 2
@@ -180,12 +206,11 @@
             out_specs=[
                 straight,
                 straight,
-                straight,
                 pl.BlockSpec((step_groups, pipes, rows, half), lambda s, o: (s, 0, 0, 0)),
                 pl.BlockSpec((expert_count, pipes, step_slots, half), lambda s, o: (0, 0, s, 0)),
             ],
         ),
-        out_shape=[jax.ShapeDtypeStruct((everything, hidden), BF16)] * 3
+        out_shape=[jax.ShapeDtypeStruct((everything, hidden), BF16)] * 2
         + [
             jax.ShapeDtypeStruct((groups, pipes, rows, half), BF16),
             jax.ShapeDtypeStruct((expert_count, pipes, everything // expert_count, half), BF16),
@@ -193,7 +218,7 @@
         compiler_params=pltpu.CompilerParams(vmem_limit_bytes=58 * MIB),
         name="expert",
         interpret=INTERPRET,
-    )(order, gate, up, x, wg, wu, wd)
+    )(order, slope, linear, x, wg, wu, wd)
 
 
 def weight_kernel(order_ref, x_ref, own_ref, before_ref, after_ref, early_ref, late_ref, act_ref, gg_ref, ug_ref, dwg_ref, dwu_ref, dwd_ref):
@@ -360,9 +385,12 @@
     near = run_stack(near)
     x = lax.all_gather(near[None], "dp", axis=0, tiled=True)
     order = (lax.axis_index("pipe") + jnp.arange(pipe_count, dtype=jnp.int32)) % pipe_count
-    gate, up = run_project(order, c, w_gate[0], w_up[0], group_count // 4)
-    act, gg, ug, ring, cross = run_expert(
-        order, gate, up, x, w_gate[0], w_up[0], w_down[0], expert_count, group_count // 4
+    gate, up = run_project(order, c[:3], w_gate[0], w_up[0], group_count // 4)
+    act, slope, linear = run_activate(
+        order, gate, up, c[3:], w_gate[0], w_up[0], group_count // 4
+    )
+    gg, ug, ring, cross = run_expert(
+        order, slope, linear, x, w_gate[0], w_up[0], w_down[0], expert_count, group_count // 4
     )
     over_groups = lax.psum_scatter(
         ring.reshape(group_count, pipe_count * slot_total, half), "dp", scatter_dimension=0, tiled=True

time: 265 us -> 263 us (level)
  waiting for transfers between devices: 121 us -> 113 us
  Pallas kernels: 39.8 us -> 44.8 us
    ppermute x15, waiting for transfers between devices: 82.3 us -> 74.5 us  [shift(): return lax.ppermute(x, axis, [(k, (k + by) % count) for k in range(count)])]
    pallas_call x0 -> x1, Pallas kernels: none -> 5.95 us  [run_activate(): pl.pallas_call(activate_kernel, grid_spec=pltpu.PrefetchScalarGridSpec(nu...]
  transfers between devices with their start and end apart: 21 -> 21, of which waited for: 14 -> 14; matrix products, arithmetic and copies ran while one was open for 1% -> 1% of each run, Pallas kernels for 9% -> 10%
where the time goes in v2:
time: 263 us; the launch traced here: 262 us
  waiting for transfers between devices  113 us (43%)
  starting transfers between devices  45.3 us (17%)
  Pallas kernels  44.8 us (17%)
  blocking collectives  40.6 us (15%)
  between operations  13.9 us (5%)
    ppermute x15, waiting for transfers between devices, shift(): return lax.ppermute(x, axis, [(k, (k + by) % count) for k in range(count)])  74.5 us
    ppermute x15, starting transfers between devices, shift(): return lax.ppermute(x, axis, [(k, (k + by) % count) for k in range(count)])  22.5 us
    all_to_all x1, blocking collectives, body(): lax.all_to_all(sent, 'expert', split_axis=0, concat_axis=0, tiled=True)  14.6 us
    pallas_call x1, Pallas kernels, run_expert(): pl.pallas_call(functools.partial(expert_kernel, expert_count), grid_spec=...  14.4 us
    all_gather x1, blocking collectives, body(): column_slots = lax.all_gather(late_index[None], 'dp', axis=0, tiled=True)  13.8 us
    reduce_scatter x1, waiting for transfers between devices, body(): lax.psum_scatter(over_groups.reshape(pipe_count, slot_total, half), 'pipe...  13.3 us
    pallas_call x1, Pallas kernels, run_weights(): pl.pallas_call(weight_kernel, grid_spec=pltpu.PrefetchScalarGridSpec(num_...  12.5 us
    all_to_all x1, blocking collectives, body(): lax.all_to_all(column, 'pipe', split_axis=0, concat_axis=0, tiled=True)  12.2 us
  transfers between devices with their start and end apart: 21, of which 14 were waited for; matrix products, arithmetic and copies ran while one was open for 1% of the time, Pallas kernels for 10%

profile of v2, /device:TPU:1, one launch (start us, length us, event | category | flops | bytes accessed | tf_op | source)
XLA Modules:
  0.0 262.0 jit_solution(5672440228296419925)
XLA Ops:
  7.2 2.0 dispatch.1
  9.2 14.6 %all_to_all.25 = bf16[8,2,16,768]{3,2,1,0:T(8,128)(2,1)S(1)} all-to-all(bf16[8,2,16,768]{3,2,1,0:T(8,128)(2,1)} %get-tuple-element.25), channel_id=1, replica_groups=mesh['expert'=8,'dp'=8,'pipe'=4] {'expert'}, dimensions={0} | all-to-all | bytes 786432 | tf_op jit(solution)/shard_map/all_to_all | solution.py:381
  23.8 2.0 collective-permute-start.12
  26.9 2.6 %collective-permute-done.12.refs_1_ = bf16[128,768]{1,0:T(8,128)(2,1)S(1)} collective-permute-done((bf16[128,768]{1,0:T(8,128)(2,1)S(1)}, bf16[128,768]{1,0:T(8,128)(2,1)S(1)}, u32[]{:S(2)}, u32[]{:S(2)}) %collective-permute-start.12) | collective-permute-done | bytes 196640 | tf_op jit(solution)/shard_map/ppermute | solution.py:311
  29.5 3.2 %collective-permute-done.13.refs_2_ = bf16[128,768]{1,0:T(8,128)(2,1)S(1)} collective-permute-done((bf16[128,768]{1,0:T(8,128)(2,1)S(1)}, bf16[128,768]{1,0:T(8,128)(2,1)S(1)}, u32[]{:S(2)}, u32[]{:S(2)}) %collective-permute-start.13) | collective-permute-done | bytes 196640 | tf_op jit(solution)/shard_map/ppermute | solution.py:311
  32.7 5.7 %collective-permute-done.14.refs_3_ = bf16[128,768]{1,0:T(8,128)(2,1)S(1)} collective-permute-done((bf16[128,768]{1,0:T(8,128)(2,1)S(1)}, bf16[128,768]{1,0:T(8,128)(2,1)S(1)}, u32[]{:S(2)}, u32[]{:S(2)}) %collective-permute-start.14) | collective-permute-done | bytes 196640 | tf_op jit(solution)/shard_map/ppermute | solution.py:311
  39.4 1.7 collective-permute-start.3
  41.1 4.0 %collective-permute-start = (bf16[128,768]{1,0:T(8,128)(2,1)S(1)}, bf16[128,768]{1,0:T(8,128)(2,1)S(1)}, u32[]{:S(2)}, u32[]{:S(2)}) collective-permute-start(bf16[128,768]{1,0:T(8,128)(2,1)S(1)} %bitcast.26), channel_id=1, source_target_pairs={{0,28},{4,0},{8,4},{12,8},{16,12},{20,16},{24,20},{28,24},{1,29},{... | collective-permute-start | bytes 589832 | tf_op jit(solution)/shard_map/ppermute | solution.py:311
  45.1 4.7 %collective-permute-done.3.refs_6_ = bf16[128,768]{1,0:T(8,128)(2,1)S(1)} collective-permute-done((bf16[128,768]{1,0:T(8,128)(2,1)S(1)}, bf16[128,768]{1,0:T(8,128)(2,1)S(1)}, u32[]{:S(2)}, u32[]{:S(2)}) %collective-permute-start.3) | collective-permute-done | bytes 196640 | tf_op jit(solution)/shard_map/ppermute | solution.py:311
  49.8 2.7 %collective-permute-start.1 = (bf16[128,768]{1,0:T(8,128)(2,1)S(1)}, bf16[128,768]{1,0:T(8,128)(2,1)S(1)}, u32[]{:S(2)}, u32[]{:S(2)}) collective-permute-start(bf16[128,768]{1,0:T(8,128)(2,1)S(1)} %collective-permute-done.refs_1_), channel_id=1, source_target_pairs={{0,28},{4,0},{8,4},{12,8},{16,12},{20,16},{24,20},{28,24},{1,29},{... | collective-permute-start | bytes 589832 | tf_op jit(solution)/shard_map/ppermute | solution.py:311
  52.5 9.0 %collective-permute-done.4.refs_5_ = bf16[128,768]{1,0:T(8,128)(2,1)S(1)} collective-permute-done((bf16[128,768]{1,0:T(8,128)(2,1)S(1)}, bf16[128,768]{1,0:T(8,128)(2,1)S(1)}, u32[]{:S(2)}, u32[]{:S(2)}) %collective-permute-start.4) | collective-permute-done | bytes 196640 | tf_op jit(solution)/shard_map/ppermute | solution.py:311
  61.5 2.7 %collective-permute-start.2 = (bf16[128,768]{1,0:T(8,128)(2,1)S(1)}, bf16[128,768]{1,0:T(8,128)(2,1)S(1)}, u32[]{:S(2)}, u32[]{:S(2)}) collective-permute-start(bf16[128,768]{1,0:T(8,128)(2,1)S(1)} %collective-permute-done.1.refs_2_), channel_id=1, source_target_pairs={{0,28},{4,0},{8,4},{12,8},{16,12},{20,16},{24,20},{28,24},{1,29},{... | collective-permute-start | bytes 589832 | tf_op jit(solution)/shard_map/ppermute | solution.py:311
  64.2 9.1 %collective-permute-done.5.refs_4_ = bf16[128,768]{1,0:T(8,128)(2,1)S(1)} collective-permute-done((bf16[128,768]{1,0:T(8,128)(2,1)S(1)}, bf16[128,768]{1,0:T(8,128)(2,1)S(1)}, u32[]{:S(2)}, u32[]{:S(2)}) %collective-permute-start.5) | collective-permute-done | bytes 196640 | tf_op jit(solution)/shard_map/ppermute | solution.py:311
  73.4 2.7 %collective-permute-start.7 = (bf16[64,768]{1,0:T(8,128)(2,1)S(1)}, bf16[64,768]{1,0:T(8,128)(2,1)S(1)}, u32[]{:S(2)}, u32[]{:S(2)}) collective-permute-start(bf16[64,768]{1,0:T(8,128)(2,1)S(1)} %slice.74), channel_id=1, source_target_pairs={{0,28},{4,0},{8,4},{12,8},{16,12},{20,16},{24,20},{28,24},{1,29},{... | collective-permute-start | bytes 294920 | tf_op jit(solution)/shard_map/ppermute | solution.py:311
  76.2 4.6 %collective-permute-done.6.refs_7_ = bf16[64,768]{1,0:T(8,128)(2,1)S(1)} collective-permute-done((bf16[64,768]{1,0:T(8,128)(2,1)S(1)}, bf16[64,768]{1,0:T(8,128)(2,1)S(1)}, u32[]{:S(2)}, u32[]{:S(2)}) %collective-permute-start.6) | collective-permute-done | bytes 98336 | tf_op jit(solution)/shard_map/ppermute | solution.py:311
  81.5 2.7 %collective-permute-start.9 = (bf16[8,128,768]{2,1,0:T(8,128)(2,1)S(1)}, bf16[8,128,768]{2,1,0:T(8,128)(2,1)S(1)}, u32[]{:S(2)}, u32[]{:S(2)}) collective-permute-start(bf16[8,128,768]{2,1,0:T(8,128)(2,1)S(1)} %place.1.refs_0_.own_ref), channel_id=1, source_target_pairs={{0,3},{1,0},{2,1},{3,2},{4,7},{5,4},{6,5},{7,6},{8,11},{9,8},{10,9... | collective-permute-start | bytes 4718600 | tf_op jit(solution)/shard_map/ppermute | solution.py:311
  84.2 31.3 %collective-permute-done.8.refs_1_.before_ref = bf16[8,128,768]{2,1,0:T(8,128)(2,1)S(1)} collective-permute-done((bf16[8,128,768]{2,1,0:T(8,128)(2,1)S(1)}, bf16[8,128,768]{2,1,0:T(8,128)(2,1)S(1)}, u32[]{:S(2)}, u32[]{:S(2)}) %collective-permute-start.8) | collective-permute-done | bytes 1572896 | tf_op jit(solution)/shard_map/ppermute | solution.py:311
  117.2 2.6 %collective-permute-start.11 = (bf16[4,128,768]{2,1,0:T(8,128)(2,1)S(1)}, bf16[4,128,768]{2,1,0:T(8,128)(2,1)S(1)}, u32[]{:S(2)}, u32[]{:S(2)}) collective-permute-start(bf16[4,128,768]{2,1,0:T(8,128)(2,1)S(1)} %slice.76), channel_id=1, source_target_pairs={{0,3},{1,0},{2,1},{3,2},{4,7},{5,4},{6,5},{7,6},{8,11},{9,8},{10,9... | collective-permute-start | bytes 2359304 | tf_op jit(solution)/shard_map/ppermute | solution.py:311
  120.4 7.7 %project.1 = (f32[1024,256]{1,0:T(8,128)}, f32[1024,256]{1,0:T(8,128)}) custom-call(s32[4]{0:T(128)} %and_select_fusion.1.order_ref, bf16[8,128,768]{2,1,0:T(8,128)(2,1)} %copy-done, bf16[8,128,768]{2,1,0:T(8,128)(2,1)} %copy-done.1, bf16[8,128,768]{2,1,0:T(8,128)(2,1)} %copy-done.2, bf16[3072,256]{1,0:T(8,128)(2,1)} %bitcast.30, bf16[3072,256]{1,0:T(8,128)(2,1)} %bitcast.33), custom_call_target="tpu_custom_call" | custom-call | tf_op jit(solution)/shard_map/project/pallas_call | solution.py:97
  128.1 3.8 %collective-permute-done.10.early_ref = bf16[4,128,768]{2,1,0:T(8,128)(2,1)S(1)} collective-permute-done((bf16[4,128,768]{2,1,0:T(8,128)(2,1)S(1)}, bf16[4,128,768]{2,1,0:T(8,128)(2,1)S(1)}, u32[]{:S(2)}, u32[]{:S(2)}) %collective-permute-start.10) | collective-permute-done | bytes 786464 | tf_op jit(solution)/shard_map/ppermute | solution.py:311
  133.3 6.0 %activate.1 = (bf16[1024,256]{1,0:T(8,128)(2,1)}, f32[1024,256]{1,0:T(8,128)}, f32[1024,256]{1,0:T(8,128)}) custom-call(s32[4]{0:T(128)} %and_select_fusion.1.order_ref, f32[1024,256]{1,0:T(8,128)} %get-tuple-element.26.gate_ref, f32[1024,256]{1,0:T(8,128)} %get-tuple-element.27.up_ref, bf16[4,128,768]{2,1,0:T(8,128)(2,1)} %copy-done.3, ...), custom_call_target="tpu_custom_call" | custom-call | tf_op jit(solution)/shard_map/activate/pallas_call | solution.py:133
  139.2 14.4 %expert.1 = (bf16[1024,256]{1,0:T(8,128)(2,1)}, bf16[1024,256]{1,0:T(8,128)(2,1)}, bf16[8,4,128,384]{3,2,1,0:T(8,128)(2,1)}, bf16[8,4,128,384]{3,2,1,0:T(8,128)(2,1)}) custom-call(s32[4]{0:T(128)} %and_select_fusion.1.order_ref, f32[1024,256]{1,0:T(8,128)} %get-tuple-element.28.slope_ref, f32[1024,256]{1,0:T(8,128)} %get-tuple-element.29.linear_ref, ...), custom_call_target="tpu_custom_call" | custom-call | tf_op jit(solution)/shard_map/expert/pallas_call | solution.py:193
  153.6 8.7 %all-to-all-start.2 = ((bf16[8,4,128,384]{3,2,1,0:T(8,128)(2,1)}), bf16[8,4,128,384]{3,2,1,0:T(8,128)(2,1)S(1)}, u32[]{:S(2)}, u32[]{:S(2)}) async-start(bf16[8,4,128,384]{3,2,1,0:T(8,128)(2,1)} %get-tuple-element.39), calls=%async_computation.4 | async-start | bytes 6291456 | tf_op jit(solution)/shard_map/all_to_all | solution.py:398
  162.4 12.5 %weights.1 = (bf16[3072,256]{1,0:T(8,128)(2,1)}, bf16[3072,256]{1,0:T(8,128)(2,1)}, bf16[256,3072]{1,0:T(8,128)(2,1)}) custom-call(s32[4]{0:T(128)} %and_select_fusion.1.order_ref, bf16[8,4,128,768]{3,2,1,0:T(8,128)(2,1)} %bitcast.29, bf16[8,128,768]{2,1,0:T(8,128)(2,1)} %copy-done, bf16[8,128,768]{2,1,0:T(8,128)(2,1)} %copy-done.1, ...), custom_call_target="tpu_custom_call" | custom-call | tf_op jit(solution)/shard_map/weights/pallas_call | solution.py:246
  174.8 13.8 %all-gather.2.slots_ref = s32[8,2,32]{2,1,0:T(2,128)S(1)} all-gather(s32[1,2,32]{2,1,0:T(2,128)S(1)} %bitcast.43), channel_id=3, replica_groups=mesh['expert'=8,'dp'=8,'pipe'=4] {'dp'}, dimensions={0}, use_global_device_ids=true | all-gather | bytes 2304 | tf_op jit(solution)/shard_map/all_gather | solution.py:400
  188.7 11.9 %reduce-scatter.3.cloned.1.call-done = bf16[1,512,384]{2,1,0:T(8,128)(2,1)} async-done(((bf16[8,512,384]{2,1,0:T(8,128)(2,1)}), bf16[1,512,384]{2,1,0:T(8,128)(2,1)}) %reduce-scatter.3.cloned.1.call-update) | async-done | bytes 393232 | tf_op jit(solution)/shard_map/reduce_scatter | solution.py:395
  201.4 12.2 %all_to_all.26 = bf16[4,256,384]{2,1,0:T(8,128)(2,1)S(1)} all-to-all(bf16[4,256,384]{2,1,0:T(8,128)(2,1)S(1)} %combine.1), channel_id=1, replica_groups=mesh['expert'=8,'dp'=8,'pipe'=4] {'pipe'}, dimensions={0} | all-to-all | bytes 1572864 | tf_op jit(solution)/shard_map/all_to_all | solution.py:409
  213.5 13.3 %reduce-scatter.5.cloned.1.call-done = bf16[1,128,384]{2,1,0:T(8,128)(2,1)} async-done(((bf16[4,128,384]{2,1,0:T(8,128)(2,1)}), bf16[1,128,384]{2,1,0:T(8,128)(2,1)}) %reduce-scatter.5.cloned.1.call-update) | async-done | bytes 98320 | tf_op jit(solution)/shard_map/reduce_scatter | solution.py:405
  226.8 7.3 %all-to-all-start.1 = ((bf16[8,16,384]{2,1,0:T(8,128)(2,1)}), bf16[8,16,384]{2,1,0:T(8,128)(2,1)S(1)}, u32[]{:S(2)}, u32[]{:S(2)}) async-start(bf16[8,16,384]{2,1,0:T(8,128)(2,1)} %bitcast.40), calls=%async_computation.3 | async-start | bytes 196608 | tf_op jit(solution)/shard_map/all_to_all | solution.py:419
  234.9 4.2 %all-to-all-done.1 = bf16[8,16,384]{2,1,0:T(8,128)(2,1)S(1)} async-done(((bf16[8,16,384]{2,1,0:T(8,128)(2,1)}), bf16[8,16,384]{2,1,0:T(8,128)(2,1)S(1)}, u32[]{:S(2)}, u32[]{:S(2)}) %all-to-all-start.1) | async-done | bytes 98336 | tf_op jit(solution)/shard_map/all_to_all | solution.py:419
  239.1 6.7 %all-to-all-start.4 = ((bf16[8,32,384]{2,1,0:T(8,128)(2,1)}), bf16[8,32,384]{2,1,0:T(8,128)(2,1)S(1)}, u32[]{:S(2)}, u32[]{:S(2)}) async-start(bf16[8,32,384]{2,1,0:T(8,128)(2,1)} %bitcast.13), calls=%async_computation.6 | async-start | bytes 393216 | tf_op jit(solution)/shard_map/all_to_all | solution.py:411
  246.0 8.8 %all-to-all-done.4 = bf16[8,32,384]{2,1,0:T(8,128)(2,1)S(1)} async-done(((bf16[8,32,384]{2,1,0:T(8,128)(2,1)}), bf16[8,32,384]{2,1,0:T(8,128)(2,1)S(1)}, u32[]{:S(2)}, u32[]{:S(2)}) %all-to-all-start.4) | async-done | bytes 196640 | tf_op jit(solution)/shard_map/all_to_all | solution.py:411
  (51 shorter events, 8.9 us)
Async XLA Ops:
  7.2 132.1 %all-gather.5.cloned.1.call-start = ((), (), s32[]{:S(2)}) async-start(), calls=%async_computation.9 | async-start | bytes 7077888 | tf_op jit(solution)/shard_map/all_gather | solution.py:386
  23.8 52.4 %copy-start.7 = (s32[8]{0:T(128)S(1)}, s32[8]{0:T(128)}, u32[]{:S(2)}) copy-start(s32[8]{0:T(128)} %constant.40.clone) | copy-start | bytes 100
  23.8 5.7 %collective-permute-start.12 = (bf16[128,768]{1,0:T(8,128)(2,1)S(1)}, bf16[128,768]{1,0:T(8,128)(2,1)S(1)}, u32[]{:S(2)}, u32[]{:S(2)}) collective-permute-start(bf16[128,768]{1,0:T(8,128)(2,1)S(1)} %bitcast.21), channel_id=1, source_target_pairs={{0,3},{1,0},{2,1},{3,2},{4,7},{5,4},{6,5},{7,6},{8,11},{9,8},{10,9... | collective-permute-start | bytes 589832 | tf_op jit(solution)/shard_map/ppermute | solution.py:311
  25.9 6.9 %collective-permute-start.13 = (bf16[128,768]{1,0:T(8,128)(2,1)S(1)}, bf16[128,768]{1,0:T(8,128)(2,1)S(1)}, u32[]{:S(2)}, u32[]{:S(2)}) collective-permute-start(bf16[128,768]{1,0:T(8,128)(2,1)S(1)} %bitcast.22), channel_id=1, source_target_pairs={{0,2},{1,3},{2,0},{3,1},{4,6},{5,7},{6,4},{7,5},{8,10},{9,11},{10,... | collective-permute-start | bytes 589832 | tf_op jit(solution)/shard_map/ppermute | solution.py:311
  26.2 12.2 %collective-permute-start.14 = (bf16[128,768]{1,0:T(8,128)(2,1)S(1)}, bf16[128,768]{1,0:T(8,128)(2,1)S(1)}, u32[]{:S(2)}, u32[]{:S(2)}) collective-permute-start(bf16[128,768]{1,0:T(8,128)(2,1)S(1)} %bitcast.23), channel_id=1, source_target_pairs={{0,1},{1,2},{2,3},{3,0},{4,5},{5,6},{6,7},{7,4},{8,9},{9,10},{10,1... | collective-permute-start | bytes 589832 | tf_op jit(solution)/shard_map/ppermute | solution.py:311
  39.4 161.3 %reduce-scatter.3.cloned.1.call-start = ((), (), s32[]{:S(2)}) async-start(), calls=%async_computation.7 | async-start | bytes 3538944 | tf_op jit(solution)/shard_map/reduce_scatter | solution.py:395
  39.4 10.4 %collective-permute-start.3 = (bf16[128,768]{1,0:T(8,128)(2,1)S(1)}, bf16[128,768]{1,0:T(8,128)(2,1)S(1)}, u32[]{:S(2)}, u32[]{:S(2)}) collective-permute-start(bf16[128,768]{1,0:T(8,128)(2,1)S(1)} %bitcast.25), channel_id=1, source_target_pairs={{0,4},{4,8},{8,12},{12,16},{16,20},{20,24},{24,28},{28,0},{1,5},{5... | collective-permute-start | bytes 589832 | tf_op jit(solution)/shard_map/ppermute | solution.py:311
  41.1 8.7 %collective-permute-start = (bf16[128,768]{1,0:T(8,128)(2,1)S(1)}, bf16[128,768]{1,0:T(8,128)(2,1)S(1)}, u32[]{:S(2)}, u32[]{:S(2)}) collective-permute-start(bf16[128,768]{1,0:T(8,128)(2,1)S(1)} %bitcast.26), channel_id=1, source_target_pairs={{0,28},{4,0},{8,4},{12,8},{16,12},{20,16},{24,20},{28,24},{1,29},{... | collective-permute-start | bytes 589832 | tf_op jit(solution)/shard_map/ppermute | solution.py:311
  49.8 11.7 %collective-permute-start.4 = (bf16[128,768]{1,0:T(8,128)(2,1)S(1)}, bf16[128,768]{1,0:T(8,128)(2,1)S(1)}, u32[]{:S(2)}, u32[]{:S(2)}) collective-permute-start(bf16[128,768]{1,0:T(8,128)(2,1)S(1)} %collective-permute-done.3.refs_6_), channel_id=1, source_target_pairs={{0,4},{4,8},{8,12},{12,16},{16,20},{20,24},{24,28},{28,0},{1,5},{5... | collective-permute-start | bytes 589832 | tf_op jit(solution)/shard_map/ppermute | solution.py:311
  49.8 11.7 %collective-permute-start.1 = (bf16[128,768]{1,0:T(8,128)(2,1)S(1)}, bf16[128,768]{1,0:T(8,128)(2,1)S(1)}, u32[]{:S(2)}, u32[]{:S(2)}) collective-permute-start(bf16[128,768]{1,0:T(8,128)(2,1)S(1)} %collective-permute-done.refs_1_), channel_id=1, source_target_pairs={{0,28},{4,0},{8,4},{12,8},{16,12},{20,16},{24,20},{28,24},{1,29},{... | collective-permute-start | bytes 589832 | tf_op jit(solution)/shard_map/ppermute | solution.py:311
  61.5 11.8 %collective-permute-start.5 = (bf16[128,768]{1,0:T(8,128)(2,1)S(1)}, bf16[128,768]{1,0:T(8,128)(2,1)S(1)}, u32[]{:S(2)}, u32[]{:S(2)}) collective-permute-start(bf16[128,768]{1,0:T(8,128)(2,1)S(1)} %collective-permute-done.4.refs_5_), channel_id=1, source_target_pairs={{0,4},{4,8},{8,12},{12,16},{16,20},{20,24},{24,28},{28,0},{1,5},{5... | collective-permute-start | bytes 589832 | tf_op jit(solution)/shard_map/ppermute | solution.py:311
  61.5 11.9 %collective-permute-start.2 = (bf16[128,768]{1,0:T(8,128)(2,1)S(1)}, bf16[128,768]{1,0:T(8,128)(2,1)S(1)}, u32[]{:S(2)}, u32[]{:S(2)}) collective-permute-start(bf16[128,768]{1,0:T(8,128)(2,1)S(1)} %collective-permute-done.1.refs_2_), channel_id=1, source_target_pairs={{0,28},{4,0},{8,4},{12,8},{16,12},{20,16},{24,20},{28,24},{1,29},{... | collective-permute-start | bytes 589832 | tf_op jit(solution)/shard_map/ppermute | solution.py:311
  73.3 7.4 %collective-permute-start.6 = (bf16[64,768]{1,0:T(8,128)(2,1)S(1)}, bf16[64,768]{1,0:T(8,128)(2,1)S(1)}, u32[]{:S(2)}, u32[]{:S(2)}) collective-permute-start(bf16[64,768]{1,0:T(8,128)(2,1)S(1)} %slice.73), channel_id=1, source_target_pairs={{0,4},{4,8},{8,12},{12,16},{16,20},{20,24},{24,28},{28,0},{1,5},{5... | collective-permute-start | bytes 294920 | tf_op jit(solution)/shard_map/ppermute | solution.py:311
  73.4 7.3 %collective-permute-start.7 = (bf16[64,768]{1,0:T(8,128)(2,1)S(1)}, bf16[64,768]{1,0:T(8,128)(2,1)S(1)}, u32[]{:S(2)}, u32[]{:S(2)}) collective-permute-start(bf16[64,768]{1,0:T(8,128)(2,1)S(1)} %slice.74), channel_id=1, source_target_pairs={{0,28},{4,0},{8,4},{12,8},{16,12},{20,16},{24,20},{28,24},{1,29},{... | collective-permute-start | bytes 294920 | tf_op jit(solution)/shard_map/ppermute | solution.py:311
  81.4 35.6 %copy-start = (bf16[8,128,768]{2,1,0:T(8,128)(2,1)}, bf16[8,128,768]{2,1,0:T(8,128)(2,1)S(1)}, u32[]{:S(2)}) copy-start(bf16[8,128,768]{2,1,0:T(8,128)(2,1)S(1)} %place.1.refs_0_.own_ref) | copy-start | bytes 4718596
  81.4 34.1 %collective-permute-start.8 = (bf16[8,128,768]{2,1,0:T(8,128)(2,1)S(1)}, bf16[8,128,768]{2,1,0:T(8,128)(2,1)S(1)}, u32[]{:S(2)}, u32[]{:S(2)}) collective-permute-start(bf16[8,128,768]{2,1,0:T(8,128)(2,1)S(1)} %place.1.refs_0_.own_ref), channel_id=1, source_target_pairs={{0,1},{1,2},{2,3},{3,0},{4,5},{5,6},{6,7},{7,4},{8,9},{9,10},{10,1... | collective-permute-start | bytes 4718600 | tf_op jit(solution)/shard_map/ppermute | solution.py:311
  81.5 34.1 %collective-permute-start.9 = (bf16[8,128,768]{2,1,0:T(8,128)(2,1)S(1)}, bf16[8,128,768]{2,1,0:T(8,128)(2,1)S(1)}, u32[]{:S(2)}, u32[]{:S(2)}) collective-permute-start(bf16[8,128,768]{2,1,0:T(8,128)(2,1)S(1)} %place.1.refs_0_.own_ref), channel_id=1, source_target_pairs={{0,3},{1,0},{2,1},{3,2},{4,7},{5,4},{6,5},{7,6},{8,11},{9,8},{10,9... | collective-permute-start | bytes 4718600 | tf_op jit(solution)/shard_map/ppermute | solution.py:311
  115.5 1.6 copy-start.1
  115.6 16.4 %collective-permute-start.10 = (bf16[4,128,768]{2,1,0:T(8,128)(2,1)S(1)}, bf16[4,128,768]{2,1,0:T(8,128)(2,1)S(1)}, u32[]{:S(2)}, u32[]{:S(2)}) collective-permute-start(bf16[4,128,768]{2,1,0:T(8,128)(2,1)S(1)} %slice.75), channel_id=1, source_target_pairs={{0,1},{1,2},{2,3},{3,0},{4,5},{5,6},{6,7},{7,4},{8,9},{9,10},{10,1... | collective-permute-start | bytes 2359304 | tf_op jit(solution)/shard_map/ppermute | solution.py:311
  115.7 1.3 copy-start.2
  117.2 15.2 %collective-permute-start.11 = (bf16[4,128,768]{2,1,0:T(8,128)(2,1)S(1)}, bf16[4,128,768]{2,1,0:T(8,128)(2,1)S(1)}, u32[]{:S(2)}, u32[]{:S(2)}) collective-permute-start(bf16[4,128,768]{2,1,0:T(8,128)(2,1)S(1)} %slice.76), channel_id=1, source_target_pairs={{0,3},{1,0},{2,1},{3,2},{4,7},{5,4},{6,5},{7,6},{8,11},{9,8},{10,9... | collective-permute-start | bytes 2359304 | tf_op jit(solution)/shard_map/ppermute | solution.py:311
  131.9 0.9 copy-start.3
  132.4 0.9 copy-start.4
  153.6 47.0 %all-to-all-start.2 = ((bf16[8,4,128,384]{3,2,1,0:T(8,128)(2,1)}), bf16[8,4,128,384]{3,2,1,0:T(8,128)(2,1)S(1)}, u32[]{:S(2)}, u32[]{:S(2)}) async-start(bf16[8,4,128,384]{3,2,1,0:T(8,128)(2,1)} %get-tuple-element.39), calls=%async_computation.4 | async-start | bytes 6291456 | tf_op jit(solution)/shard_map/all_to_all | solution.py:398
  162.4 64.4 %reduce-scatter.5.cloned.1.call-start = ((), (), s32[]{:S(2)}) async-start(), calls=%async_computation.8 | async-start | bytes 491520 | tf_op jit(solution)/shard_map/reduce_scatter | solution.py:405
  162.4 12.5 %copy-start.6 = (s32[2,32]{1,0:T(2,128)S(1)}, s32[2,32]{1,0:T(2,128)}, u32[]{:S(2)}) copy-start(s32[2,32]{1,0:T(2,128)} %get-tuple-element.33) | copy-start | bytes 772
  201.3 44.5 %copy-start.5 = (bf16[128,32]{1,0:T(8,128)(2,1)S(1)}, bf16[128,32]{1,0:T(8,128)(2,1)}, u32[]{:S(2)}) copy-start(bf16[128,32]{1,0:T(8,128)(2,1)} %get-tuple-element.24) | copy-start | bytes 24580
  226.8 12.3 %all-to-all-start.1 = ((bf16[8,16,384]{2,1,0:T(8,128)(2,1)}), bf16[8,16,384]{2,1,0:T(8,128)(2,1)S(1)}, u32[]{:S(2)}, u32[]{:S(2)}) async-start(bf16[8,16,384]{2,1,0:T(8,128)(2,1)} %bitcast.40), calls=%async_computation.3 | async-start | bytes 196608 | tf_op jit(solution)/shard_map/all_to_all | solution.py:419
  239.1 15.7 %all-to-all-start.4 = ((bf16[8,32,384]{2,1,0:T(8,128)(2,1)}), bf16[8,32,384]{2,1,0:T(8,128)(2,1)S(1)}, u32[]{:S(2)}, u32[]{:S(2)}) async-start(bf16[8,32,384]{2,1,0:T(8,128)(2,1)} %bitcast.13), calls=%async_computation.6 | async-start | bytes 393216 | tf_op jit(solution)/shard_map/all_to_all | solution.py:411
Sparse Core Ops, SparseCore 0:
  39.5 83.1 all-gather.4
  153.8 46.7 reduce-scatter.2
  203.1 23.6 reduce-scatter.4

commit v3 on v2

--- a/solution.py
+++ b/solution.py
@@ -19,6 +19,10 @@
 
 def dot(a, b, dims=NN):
     return lax.dot_general(a, b, dims, preferred_element_type=F32)
+
+
+def in_hbm(shape, dtype):
+    return jax.ShapeDtypeStruct(shape, dtype) if INTERPRET else pltpu.HBM(shape, dtype)
 
 
 def dispatch_kernel(expert_count, ids_ref, gates_ref, g_ref, *refs):
@@ -103,7 +107,7 @@
             out_specs=[result, result],
         ),
         out_shape=[jax.ShapeDtypeStruct((groups * rows, hidden), F32)] * 2,
-        compiler_params=pltpu.CompilerParams(vmem_limit_bytes=58 * MIB),
+        compiler_params=pltpu.CompilerParams(vmem_limit_bytes=40 * MIB),
         name="project",
         interpret=INTERPRET,
     )(order, *c, wg, wu)
@@ -146,11 +150,11 @@
             out_specs=[straight, straight, straight],
         ),
         out_shape=[
-            jax.ShapeDtypeStruct((everything, hidden), BF16),
-            jax.ShapeDtypeStruct((everything, hidden), F32),
-            jax.ShapeDtypeStruct((everything, hidden), F32),
+            in_hbm((everything, hidden), BF16),
+            in_hbm((everything, hidden), F32),
+            in_hbm((everything, hidden), F32),
         ],
-        compiler_params=pltpu.CompilerParams(vmem_limit_bytes=58 * MIB),
+        compiler_params=pltpu.CompilerParams(vmem_limit_bytes=24 * MIB),
         name="activate",
         interpret=INTERPRET,
     )(order, gate, up, *far, wg, wu)
@@ -387,7 +391,7 @@
     order = (lax.axis_index("pipe") + jnp.arange(pipe_count, dtype=jnp.int32)) % pipe_count
     gate, up = run_project(order, c[:3], w_gate[0], w_up[0], group_count // 4)
     act, slope, linear = run_activate(
-        order, gate, up, c[3:], w_gate[0], w_up[0], group_count // 4
+        order, gate, up, c[3:], w_gate[0], w_up[0], group_count // 2
     )
     gg, ug, ring, cross = run_expert(
         order, slope, linear, x, w_gate[0], w_up[0], w_down[0], expert_count, group_count // 4

time: 263 us -> 262 us (level)
  Pallas kernels: 44.8 us -> 39.1 us
  local copies, waits for them, and re-layouts: 2.48 us -> 7.41 us
    pallas_call x1, Pallas kernels: 7.73 us -> 3.69 us  [run_project(): pl.pallas_call(project_kernel, grid_spec=pltpu.PrefetchScalarGridSpec(num...]
    unnamed x16 -> x24, local copies, waits for them, and re-layouts: 2.33 us -> 5.41 us
  transfers between devices with their start and end apart: 21 -> 21, of which waited for: 14 -> 14; matrix products, arithmetic and copies ran while one was open for 1% -> 1% of each run, Pallas kernels for 10% -> 8%
where the time goes in v3:
time: 262 us; the launch traced here: 261 us
  waiting for transfers between devices  113 us (43%)
  starting transfers between devices  45.3 us (17%)
  blocking collectives  40.6 us (15%)
  Pallas kernels  39.1 us (15%)
  between operations  13.9 us (5%)
  local copies, waits for them, and re-layouts  7.41 us (3%)
    ppermute x15, waiting for transfers between devices, shift(): return lax.ppermute(x, axis, [(k, (k + by) % count) for k in range(count)])  75.2 us
    ppermute x15, starting transfers between devices, shift(): return lax.ppermute(x, axis, [(k, (k + by) % count) for k in range(count)])  22.4 us
    all_to_all x1, blocking collectives, body(): lax.all_to_all(sent, 'expert', split_axis=0, concat_axis=0, tiled=True)  14.6 us
    pallas_call x1, Pallas kernels, run_expert(): pl.pallas_call(functools.partial(expert_kernel, expert_count), grid_spec=...  14.4 us
    all_gather x1, blocking collectives, body(): column_slots = lax.all_gather(late_index[None], 'dp', axis=0, tiled=True)  13.8 us
    reduce_scatter x1, waiting for transfers between devices, body(): lax.psum_scatter(over_groups.reshape(pipe_count, slot_total, half), 'pipe...  13.4 us
    pallas_call x1, Pallas kernels, run_weights(): pl.pallas_call(weight_kernel, grid_spec=pltpu.PrefetchScalarGridSpec(num_...  12.5 us
    all_to_all x1, blocking collectives, body(): lax.all_to_all(column, 'pipe', split_axis=0, concat_axis=0, tiled=True)  12.2 us
  transfers between devices with their start and end apart: 21, of which 14 were waited for; matrix products, arithmetic and copies ran while one was open for 1% of the time, Pallas kernels for 8%

profile of v3, /device:TPU:1, one launch (start us, length us, event | category | flops | bytes accessed | tf_op | source)
XLA Modules:
  0.0 261.5 jit_solution(5513591280755337432)
XLA Ops:
  7.2 2.0 dispatch.1
  9.2 14.6 %all_to_all.25 = bf16[8,2,16,768]{3,2,1,0:T(8,128)(2,1)S(1)} all-to-all(bf16[8,2,16,768]{3,2,1,0:T(8,128)(2,1)} %get-tuple-element.25), channel_id=1, replica_groups=mesh['expert'=8,'dp'=8,'pipe'=4] {'expert'}, dimensions={0} | all-to-all | bytes 786432 | tf_op jit(solution)/shard_map/all_to_all | solution.py:385
  23.8 2.0 collective-permute-start.12
  26.9 2.6 %collective-permute-done.12.refs_1_ = bf16[128,768]{1,0:T(8,128)(2,1)S(1)} collective-permute-done((bf16[128,768]{1,0:T(8,128)(2,1)S(1)}, bf16[128,768]{1,0:T(8,128)(2,1)S(1)}, u32[]{:S(2)}, u32[]{:S(2)}) %collective-permute-start.12) | collective-permute-done | bytes 196640 | tf_op jit(solution)/shard_map/ppermute | solution.py:315
  29.5 3.2 %collective-permute-done.13.refs_2_ = bf16[128,768]{1,0:T(8,128)(2,1)S(1)} collective-permute-done((bf16[128,768]{1,0:T(8,128)(2,1)S(1)}, bf16[128,768]{1,0:T(8,128)(2,1)S(1)}, u32[]{:S(2)}, u32[]{:S(2)}) %collective-permute-start.13) | collective-permute-done | bytes 196640 | tf_op jit(solution)/shard_map/ppermute | solution.py:315
  32.7 5.7 %collective-permute-done.14.refs_3_ = bf16[128,768]{1,0:T(8,128)(2,1)S(1)} collective-permute-done((bf16[128,768]{1,0:T(8,128)(2,1)S(1)}, bf16[128,768]{1,0:T(8,128)(2,1)S(1)}, u32[]{:S(2)}, u32[]{:S(2)}) %collective-permute-start.14) | collective-permute-done | bytes 196640 | tf_op jit(solution)/shard_map/ppermute | solution.py:315
  39.4 1.7 collective-permute-start.3
  41.1 4.0 %collective-permute-start = (bf16[128,768]{1,0:T(8,128)(2,1)S(1)}, bf16[128,768]{1,0:T(8,128)(2,1)S(1)}, u32[]{:S(2)}, u32[]{:S(2)}) collective-permute-start(bf16[128,768]{1,0:T(8,128)(2,1)S(1)} %bitcast.32), channel_id=1, source_target_pairs={{0,28},{4,0},{8,4},{12,8},{16,12},{20,16},{24,20},{28,24},{1,29},{... | collective-permute-start | bytes 589832 | tf_op jit(solution)/shard_map/ppermute | solution.py:315
  45.1 4.7 %collective-permute-done.3.refs_6_ = bf16[128,768]{1,0:T(8,128)(2,1)S(1)} collective-permute-done((bf16[128,768]{1,0:T(8,128)(2,1)S(1)}, bf16[128,768]{1,0:T(8,128)(2,1)S(1)}, u32[]{:S(2)}, u32[]{:S(2)}) %collective-permute-start.3) | collective-permute-done | bytes 196640 | tf_op jit(solution)/shard_map/ppermute | solution.py:315
  49.8 2.7 %collective-permute-start.1 = (bf16[128,768]{1,0:T(8,128)(2,1)S(1)}, bf16[128,768]{1,0:T(8,128)(2,1)S(1)}, u32[]{:S(2)}, u32[]{:S(2)}) collective-permute-start(bf16[128,768]{1,0:T(8,128)(2,1)S(1)} %collective-permute-done.refs_1_), channel_id=1, source_target_pairs={{0,28},{4,0},{8,4},{12,8},{16,12},{20,16},{24,20},{28,24},{1,29},{... | collective-permute-start | bytes 589832 | tf_op jit(solution)/shard_map/ppermute | solution.py:315
  52.5 9.0 %collective-permute-done.4.refs_5_ = bf16[128,768]{1,0:T(8,128)(2,1)S(1)} collective-permute-done((bf16[128,768]{1,0:T(8,128)(2,1)S(1)}, bf16[128,768]{1,0:T(8,128)(2,1)S(1)}, u32[]{:S(2)}, u32[]{:S(2)}) %collective-permute-start.4) | collective-permute-done | bytes 196640 | tf_op jit(solution)/shard_map/ppermute | solution.py:315
  61.5 2.7 %collective-permute-start.2 = (bf16[128,768]{1,0:T(8,128)(2,1)S(1)}, bf16[128,768]{1,0:T(8,128)(2,1)S(1)}, u32[]{:S(2)}, u32[]{:S(2)}) collective-permute-start(bf16[128,768]{1,0:T(8,128)(2,1)S(1)} %collective-permute-done.1.refs_2_), channel_id=1, source_target_pairs={{0,28},{4,0},{8,4},{12,8},{16,12},{20,16},{24,20},{28,24},{1,29},{... | collective-permute-start | bytes 589832 | tf_op jit(solution)/shard_map/ppermute | solution.py:315
  64.2 9.1 %collective-permute-done.5.refs_4_ = bf16[128,768]{1,0:T(8,128)(2,1)S(1)} collective-permute-done((bf16[128,768]{1,0:T(8,128)(2,1)S(1)}, bf16[128,768]{1,0:T(8,128)(2,1)S(1)}, u32[]{:S(2)}, u32[]{:S(2)}) %collective-permute-start.5) | collective-permute-done | bytes 196640 | tf_op jit(solution)/shard_map/ppermute | solution.py:315
  73.4 2.7 %collective-permute-start.7 = (bf16[64,768]{1,0:T(8,128)(2,1)S(1)}, bf16[64,768]{1,0:T(8,128)(2,1)S(1)}, u32[]{:S(2)}, u32[]{:S(2)}) collective-permute-start(bf16[64,768]{1,0:T(8,128)(2,1)S(1)} %slice.74), channel_id=1, source_target_pairs={{0,28},{4,0},{8,4},{12,8},{16,12},{20,16},{24,20},{28,24},{1,29},{... | collective-permute-start | bytes 294920 | tf_op jit(solution)/shard_map/ppermute | solution.py:315
  76.2 4.6 %collective-permute-done.6.refs_7_ = bf16[64,768]{1,0:T(8,128)(2,1)S(1)} collective-permute-done((bf16[64,768]{1,0:T(8,128)(2,1)S(1)}, bf16[64,768]{1,0:T(8,128)(2,1)S(1)}, u32[]{:S(2)}, u32[]{:S(2)}) %collective-permute-start.6) | collective-permute-done | bytes 98336 | tf_op jit(solution)/shard_map/ppermute | solution.py:315
  81.5 2.7 %collective-permute-start.9 = (bf16[8,128,768]{2,1,0:T(8,128)(2,1)S(1)}, bf16[8,128,768]{2,1,0:T(8,128)(2,1)S(1)}, u32[]{:S(2)}, u32[]{:S(2)}) collective-permute-start(bf16[8,128,768]{2,1,0:T(8,128)(2,1)S(1)} %place.1.refs_0_.own_ref), channel_id=1, source_target_pairs={{0,3},{1,0},{2,1},{3,2},{4,7},{5,4},{6,5},{7,6},{8,11},{9,8},{10,9... | collective-permute-start | bytes 4718600 | tf_op jit(solution)/shard_map/ppermute | solution.py:315
  84.2 31.3 %collective-permute-done.8.refs_1_.before_ref = bf16[8,128,768]{2,1,0:T(8,128)(2,1)S(1)} collective-permute-done((bf16[8,128,768]{2,1,0:T(8,128)(2,1)S(1)}, bf16[8,128,768]{2,1,0:T(8,128)(2,1)S(1)}, u32[]{:S(2)}, u32[]{:S(2)}) %collective-permute-start.8) | collective-permute-done | bytes 1572896 | tf_op jit(solution)/shard_map/ppermute | solution.py:315
  118.7 2.7 %collective-permute-start.11 = (bf16[4,128,768]{2,1,0:T(8,128)(2,1)}, bf16[4,128,768]{2,1,0:T(8,128)(2,1)}, u32[]{:S(2)}, u32[]{:S(2)}) collective-permute-start(bf16[4,128,768]{2,1,0:T(8,128)(2,1)} %slice.76), channel_id=1, source_target_pairs={{0,3},{1,0},{2,1},{3,2},{4,7},{5,4},{6,5},{7,6},{8,11},{9,8},{10,9... | collective-permute-start | bytes 2359304 | tf_op jit(solution)/shard_map/ppermute | solution.py:315
  125.6 3.7 %project.1 = (f32[1024,256]{1,0:T(8,128)S(1)}, f32[1024,256]{1,0:T(8,128)S(1)}) custom-call(s32[4]{0:T(128)S(1)} %and_select_fusion.1.order_ref, bf16[8,128,768]{2,1,0:T(8,128)(2,1)S(1)} %copy-done.3, bf16[8,128,768]{2,1,0:T(8,128)(2,1)S(1)} %copy-done.5, bf16[8,128,768]{2,1,0:T(8,128)(2,1)S(1)} %copy-done.7, bf16[3072,256]{1,0:T(8,128)(2,1)S(1)} %bitcast.22, ...), custom_call_target="tpu_custom_call" | custom-call | tf_op jit(solution)/shard_map/project/pallas_call | solution.py:101
  129.3 3.9 %collective-permute-done.10.early_ref = bf16[4,128,768]{2,1,0:T(8,128)(2,1)} collective-permute-done((bf16[4,128,768]{2,1,0:T(8,128)(2,1)}, bf16[4,128,768]{2,1,0:T(8,128)(2,1)}, u32[]{:S(2)}, u32[]{:S(2)}) %collective-permute-start.10) | collective-permute-done | bytes 786464 | tf_op jit(solution)/shard_map/ppermute | solution.py:315
  134.3 4.4 %activate.1 = (bf16[1024,256]{1,0:T(8,128)(2,1)}, f32[1024,256]{1,0:T(8,128)}, f32[1024,256]{1,0:T(8,128)}) custom-call(s32[4]{0:T(128)S(1)} %and_select_fusion.1.order_ref, f32[1024,256]{1,0:T(8,128)S(1)} %get-tuple-element.26.gate_ref, f32[1024,256]{1,0:T(8,128)S(1)} %get-tuple-element.27.up_ref, bf16[4,128,768]{2,1,0:T(8,128)(2,1)} %collective-permute-done.10.early_ref, ...), custom_call_target="tpu_custom_call" | custom-call | tf_op jit(solution)/shard_map/activate/pallas_call | solution.py:137
  138.6 14.4 %expert.1 = (bf16[1024,256]{1,0:T(8,128)(2,1)}, bf16[1024,256]{1,0:T(8,128)(2,1)}, bf16[8,4,128,384]{3,2,1,0:T(8,128)(2,1)}, bf16[8,4,128,384]{3,2,1,0:T(8,128)(2,1)}) custom-call(s32[4]{0:T(128)} %copy-done.8, f32[1024,256]{1,0:T(8,128)} %get-tuple-element.28.slope_ref, f32[1024,256]{1,0:T(8,128)} %get-tuple-element.29.linear_ref, ...), custom_call_target="tpu_custom_call" | custom-call | tf_op jit(solution)/shard_map/expert/pallas_call | solution.py:197
  153.0 8.7 %all-to-all-start.2 = ((bf16[8,4,128,384]{3,2,1,0:T(8,128)(2,1)}), bf16[8,4,128,384]{3,2,1,0:T(8,128)(2,1)S(1)}, u32[]{:S(2)}, u32[]{:S(2)}) async-start(bf16[8,4,128,384]{3,2,1,0:T(8,128)(2,1)} %get-tuple-element.39), calls=%async_computation.4 | async-start | bytes 6291456 | tf_op jit(solution)/shard_map/all_to_all | solution.py:402
  161.8 12.5 %weights.1 = (bf16[3072,256]{1,0:T(8,128)(2,1)}, bf16[3072,256]{1,0:T(8,128)(2,1)}, bf16[256,3072]{1,0:T(8,128)(2,1)}) custom-call(s32[4]{0:T(128)} %copy-done.8, bf16[8,4,128,768]{3,2,1,0:T(8,128)(2,1)} %bitcast.35, bf16[8,128,768]{2,1,0:T(8,128)(2,1)} %copy-done.2, bf16[8,128,768]{2,1,0:T(8,128)(2,1)} %copy-done.4, bf16[8,128,768]{2,1,0:T(8,128)(2,1)} %copy-done.6, ...), custom_call_target="tpu_custom_call" | custom-call | tf_op jit(solution)/shard_map/weights/pallas_call | solution.py:250
  174.2 13.8 %all-gather.2.slots_ref = s32[8,2,32]{2,1,0:T(2,128)S(1)} all-gather(s32[1,2,32]{2,1,0:T(2,128)S(1)} %bitcast.43), channel_id=3, replica_groups=mesh['expert'=8,'dp'=8,'pipe'=4] {'dp'}, dimensions={0}, use_global_device_ids=true | all-gather | bytes 2304 | tf_op jit(solution)/shard_map/all_gather | solution.py:404
  188.1 11.8 %reduce-scatter.3.cloned.1.call-done = bf16[1,512,384]{2,1,0:T(8,128)(2,1)} async-done(((bf16[8,512,384]{2,1,0:T(8,128)(2,1)}), bf16[1,512,384]{2,1,0:T(8,128)(2,1)}) %reduce-scatter.3.cloned.1.call-update) | async-done | bytes 393232 | tf_op jit(solution)/shard_map/reduce_scatter | solution.py:399
  200.7 12.2 %all_to_all.26 = bf16[4,256,384]{2,1,0:T(8,128)(2,1)S(1)} all-to-all(bf16[4,256,384]{2,1,0:T(8,128)(2,1)S(1)} %combine.1), channel_id=1, replica_groups=mesh['expert'=8,'dp'=8,'pipe'=4] {'pipe'}, dimensions={0} | all-to-all | bytes 1572864 | tf_op jit(solution)/shard_map/all_to_all | solution.py:413
  212.9 13.4 %reduce-scatter.5.cloned.1.call-done = bf16[1,128,384]{2,1,0:T(8,128)(2,1)} async-done(((bf16[4,128,384]{2,1,0:T(8,128)(2,1)}), bf16[1,128,384]{2,1,0:T(8,128)(2,1)}) %reduce-scatter.5.cloned.1.call-update) | async-done | bytes 98320 | tf_op jit(solution)/shard_map/reduce_scatter | solution.py:409
  226.2 7.3 %all-to-all-start.1 = ((bf16[8,16,384]{2,1,0:T(8,128)(2,1)}), bf16[8,16,384]{2,1,0:T(8,128)(2,1)S(1)}, u32[]{:S(2)}, u32[]{:S(2)}) async-start(bf16[8,16,384]{2,1,0:T(8,128)(2,1)} %bitcast.40), calls=%async_computation.3 | async-start | bytes 196608 | tf_op jit(solution)/shard_map/all_to_all | solution.py:423
  234.4 4.2 %all-to-all-done.1 = bf16[8,16,384]{2,1,0:T(8,128)(2,1)S(1)} async-done(((bf16[8,16,384]{2,1,0:T(8,128)(2,1)}), bf16[8,16,384]{2,1,0:T(8,128)(2,1)S(1)}, u32[]{:S(2)}, u32[]{:S(2)}) %all-to-all-start.1) | async-done | bytes 98336 | tf_op jit(solution)/shard_map/all_to_all | solution.py:423
  238.6 6.7 %all-to-all-start.4 = ((bf16[8,32,384]{2,1,0:T(8,128)(2,1)}), bf16[8,32,384]{2,1,0:T(8,128)(2,1)S(1)}, u32[]{:S(2)}, u32[]{:S(2)}) async-start(bf16[8,32,384]{2,1,0:T(8,128)(2,1)} %bitcast.13), calls=%async_computation.6 | async-start | bytes 393216 | tf_op jit(solution)/shard_map/all_to_all | solution.py:415
  245.5 8.8 %all-to-all-done.4 = bf16[8,32,384]{2,1,0:T(8,128)(2,1)S(1)} async-done(((bf16[8,32,384]{2,1,0:T(8,128)(2,1)}), bf16[8,32,384]{2,1,0:T(8,128)(2,1)S(1)}, u32[]{:S(2)}, u32[]{:S(2)}) %all-to-all-start.4) | async-done | bytes 196640 | tf_op jit(solution)/shard_map/all_to_all | solution.py:415
  (59 shorter events, 13.8 us)
Async XLA Ops:
  7.2 131.5 %all-gather.5.cloned.1.call-start = ((), (), s32[]{:S(2)}) async-start(), calls=%async_computation.9 | async-start | bytes 7077888 | tf_op jit(solution)/shard_map/all_gather | solution.py:390
  23.8 52.4 %copy-start.11 = (s32[8]{0:T(128)S(1)}, s32[8]{0:T(128)}, u32[]{:S(2)}) copy-start(s32[8]{0:T(128)} %constant.40.clone) | copy-start | bytes 100
  23.8 5.7 %collective-permute-start.12 = (bf16[128,768]{1,0:T(8,128)(2,1)S(1)}, bf16[128,768]{1,0:T(8,128)(2,1)S(1)}, u32[]{:S(2)}, u32[]{:S(2)}) collective-permute-start(bf16[128,768]{1,0:T(8,128)(2,1)S(1)} %bitcast.27), channel_id=1, source_target_pairs={{0,3},{1,0},{2,1},{3,2},{4,7},{5,4},{6,5},{7,6},{8,11},{9,8},{10,9... | collective-permute-start | bytes 589832 | tf_op jit(solution)/shard_map/ppermute | solution.py:315
  25.9 6.9 %collective-permute-start.13 = (bf16[128,768]{1,0:T(8,128)(2,1)S(1)}, bf16[128,768]{1,0:T(8,128)(2,1)S(1)}, u32[]{:S(2)}, u32[]{:S(2)}) collective-permute-start(bf16[128,768]{1,0:T(8,128)(2,1)S(1)} %bitcast.28), channel_id=1, source_target_pairs={{0,2},{1,3},{2,0},{3,1},{4,6},{5,7},{6,4},{7,5},{8,10},{9,11},{10,... | collective-permute-start | bytes 589832 | tf_op jit(solution)/shard_map/ppermute | solution.py:315
  26.2 12.2 %collective-permute-start.14 = (bf16[128,768]{1,0:T(8,128)(2,1)S(1)}, bf16[128,768]{1,0:T(8,128)(2,1)S(1)}, u32[]{:S(2)}, u32[]{:S(2)}) collective-permute-start(bf16[128,768]{1,0:T(8,128)(2,1)S(1)} %bitcast.29), channel_id=1, source_target_pairs={{0,1},{1,2},{2,3},{3,0},{4,5},{5,6},{6,7},{7,4},{8,9},{9,10},{10,1... | collective-permute-start | bytes 589832 | tf_op jit(solution)/shard_map/ppermute | solution.py:315
  39.4 160.6 %reduce-scatter.3.cloned.1.call-start = ((), (), s32[]{:S(2)}) async-start(), calls=%async_computation.7 | async-start | bytes 3538944 | tf_op jit(solution)/shard_map/reduce_scatter | solution.py:399
  39.4 10.4 %collective-permute-start.3 = (bf16[128,768]{1,0:T(8,128)(2,1)S(1)}, bf16[128,768]{1,0:T(8,128)(2,1)S(1)}, u32[]{:S(2)}, u32[]{:S(2)}) collective-permute-start(bf16[128,768]{1,0:T(8,128)(2,1)S(1)} %bitcast.31), channel_id=1, source_target_pairs={{0,4},{4,8},{8,12},{12,16},{16,20},{20,24},{24,28},{28,0},{1,5},{5... | collective-permute-start | bytes 589832 | tf_op jit(solution)/shard_map/ppermute | solution.py:315
  41.1 8.7 %collective-permute-start = (bf16[128,768]{1,0:T(8,128)(2,1)S(1)}, bf16[128,768]{1,0:T(8,128)(2,1)S(1)}, u32[]{:S(2)}, u32[]{:S(2)}) collective-permute-start(bf16[128,768]{1,0:T(8,128)(2,1)S(1)} %bitcast.32), channel_id=1, source_target_pairs={{0,28},{4,0},{8,4},{12,8},{16,12},{20,16},{24,20},{28,24},{1,29},{... | collective-permute-start | bytes 589832 | tf_op jit(solution)/shard_map/ppermute | solution.py:315
  49.8 11.7 %collective-permute-start.4 = (bf16[128,768]{1,0:T(8,128)(2,1)S(1)}, bf16[128,768]{1,0:T(8,128)(2,1)S(1)}, u32[]{:S(2)}, u32[]{:S(2)}) collective-permute-start(bf16[128,768]{1,0:T(8,128)(2,1)S(1)} %collective-permute-done.3.refs_6_), channel_id=1, source_target_pairs={{0,4},{4,8},{8,12},{12,16},{16,20},{20,24},{24,28},{28,0},{1,5},{5... | collective-permute-start | bytes 589832 | tf_op jit(solution)/shard_map/ppermute | solution.py:315
  49.8 11.7 %collective-permute-start.1 = (bf16[128,768]{1,0:T(8,128)(2,1)S(1)}, bf16[128,768]{1,0:T(8,128)(2,1)S(1)}, u32[]{:S(2)}, u32[]{:S(2)}) collective-permute-start(bf16[128,768]{1,0:T(8,128)(2,1)S(1)} %collective-permute-done.refs_1_), channel_id=1, source_target_pairs={{0,28},{4,0},{8,4},{12,8},{16,12},{20,16},{24,20},{28,24},{1,29},{... | collective-permute-start | bytes 589832 | tf_op jit(solution)/shard_map/ppermute | solution.py:315
  61.5 11.8 %collective-permute-start.5 = (bf16[128,768]{1,0:T(8,128)(2,1)S(1)}, bf16[128,768]{1,0:T(8,128)(2,1)S(1)}, u32[]{:S(2)}, u32[]{:S(2)}) collective-permute-start(bf16[128,768]{1,0:T(8,128)(2,1)S(1)} %collective-permute-done.4.refs_5_), channel_id=1, source_target_pairs={{0,4},{4,8},{8,12},{12,16},{16,20},{20,24},{24,28},{28,0},{1,5},{5... | collective-permute-start | bytes 589832 | tf_op jit(solution)/shard_map/ppermute | solution.py:315
  61.5 11.9 %collective-permute-start.2 = (bf16[128,768]{1,0:T(8,128)(2,1)S(1)}, bf16[128,768]{1,0:T(8,128)(2,1)S(1)}, u32[]{:S(2)}, u32[]{:S(2)}) collective-permute-start(bf16[128,768]{1,0:T(8,128)(2,1)S(1)} %collective-permute-done.1.refs_2_), channel_id=1, source_target_pairs={{0,28},{4,0},{8,4},{12,8},{16,12},{20,16},{24,20},{28,24},{1,29},{... | collective-permute-start | bytes 589832 | tf_op jit(solution)/shard_map/ppermute | solution.py:315
  73.3 7.4 %collective-permute-start.6 = (bf16[64,768]{1,0:T(8,128)(2,1)S(1)}, bf16[64,768]{1,0:T(8,128)(2,1)S(1)}, u32[]{:S(2)}, u32[]{:S(2)}) collective-permute-start(bf16[64,768]{1,0:T(8,128)(2,1)S(1)} %slice.73), channel_id=1, source_target_pairs={{0,4},{4,8},{8,12},{12,16},{16,20},{20,24},{24,28},{28,0},{1,5},{5... | collective-permute-start | bytes 294920 | tf_op jit(solution)/shard_map/ppermute | solution.py:315
  73.4 7.3 %collective-permute-start.7 = (bf16[64,768]{1,0:T(8,128)(2,1)S(1)}, bf16[64,768]{1,0:T(8,128)(2,1)S(1)}, u32[]{:S(2)}, u32[]{:S(2)}) collective-permute-start(bf16[64,768]{1,0:T(8,128)(2,1)S(1)} %slice.74), channel_id=1, source_target_pairs={{0,28},{4,0},{8,4},{12,8},{16,12},{20,16},{24,20},{28,24},{1,29},{... | collective-permute-start | bytes 294920 | tf_op jit(solution)/shard_map/ppermute | solution.py:315
  81.4 36.1 %copy-start.2 = (bf16[8,128,768]{2,1,0:T(8,128)(2,1)}, bf16[8,128,768]{2,1,0:T(8,128)(2,1)S(1)}, u32[]{:S(2)}) copy-start(bf16[8,128,768]{2,1,0:T(8,128)(2,1)S(1)} %place.1.refs_0_.own_ref) | copy-start | bytes 4718596
  81.4 39.9 %copy-start = (bf16[1,3072,256]{2,1,0:T(8,128)(2,1)S(1)}, bf16[1,3072,256]{2,1,0:T(8,128)(2,1)}, u32[]{:S(2)}) copy-start(bf16[1,3072,256]{2,1,0:T(8,128)(2,1)} %param.12) | copy-start | bytes 4718596
  81.4 39.9 %copy-start.1 = (bf16[1,3072,256]{2,1,0:T(8,128)(2,1)S(1)}, bf16[1,3072,256]{2,1,0:T(8,128)(2,1)}, u32[]{:S(2)}) copy-start(bf16[1,3072,256]{2,1,0:T(8,128)(2,1)} %param.13) | copy-start | bytes 4718596
  81.5 34.1 %collective-permute-start.8 = (bf16[8,128,768]{2,1,0:T(8,128)(2,1)S(1)}, bf16[8,128,768]{2,1,0:T(8,128)(2,1)S(1)}, u32[]{:S(2)}, u32[]{:S(2)}) collective-permute-start(bf16[8,128,768]{2,1,0:T(8,128)(2,1)S(1)} %place.1.refs_0_.own_ref), channel_id=1, source_target_pairs={{0,1},{1,2},{2,3},{3,0},{4,5},{5,6},{6,7},{7,4},{8,9},{9,10},{10,1... | collective-permute-start | bytes 4718600 | tf_op jit(solution)/shard_map/ppermute | solution.py:315
  81.5 35.0 %collective-permute-start.9 = (bf16[8,128,768]{2,1,0:T(8,128)(2,1)S(1)}, bf16[8,128,768]{2,1,0:T(8,128)(2,1)S(1)}, u32[]{:S(2)}, u32[]{:S(2)}) collective-permute-start(bf16[8,128,768]{2,1,0:T(8,128)(2,1)S(1)} %place.1.refs_0_.own_ref), channel_id=1, source_target_pairs={{0,3},{1,0},{2,1},{3,2},{4,7},{5,4},{6,5},{7,6},{8,11},{9,8},{10,9... | collective-permute-start | bytes 4718600 | tf_op jit(solution)/shard_map/ppermute | solution.py:315
  115.5 2.0 copy-start.4
  116.6 16.6 %collective-permute-start.10 = (bf16[4,128,768]{2,1,0:T(8,128)(2,1)}, bf16[4,128,768]{2,1,0:T(8,128)(2,1)}, u32[]{:S(2)}, u32[]{:S(2)}) collective-permute-start(bf16[4,128,768]{2,1,0:T(8,128)(2,1)} %slice.75), channel_id=1, source_target_pairs={{0,1},{1,2},{2,3},{3,0},{4,5},{5,6},{6,7},{7,4},{8,9},{9,10},{10,1... | collective-permute-start | bytes 2359304 | tf_op jit(solution)/shard_map/ppermute | solution.py:315
  118.7 15.6 %collective-permute-start.11 = (bf16[4,128,768]{2,1,0:T(8,128)(2,1)}, bf16[4,128,768]{2,1,0:T(8,128)(2,1)}, u32[]{:S(2)}, u32[]{:S(2)}) collective-permute-start(bf16[4,128,768]{2,1,0:T(8,128)(2,1)} %slice.76), channel_id=1, source_target_pairs={{0,3},{1,0},{2,1},{3,2},{4,7},{5,4},{6,5},{7,6},{8,11},{9,8},{10,9... | collective-permute-start | bytes 2359304 | tf_op jit(solution)/shard_map/ppermute | solution.py:315
  121.3 12.9 %copy-start.8 = (s32[4]{0:T(128)}, s32[4]{0:T(128)S(1)}, u32[]{:S(2)}) copy-start(s32[4]{0:T(128)S(1)} %and_select_fusion.1.order_ref) | copy-start | bytes 52
  121.4 1.4 copy-start.3
  122.8 1.4 copy-start.5
  124.2 1.4 copy-start.7
  153.0 46.9 %all-to-all-start.2 = ((bf16[8,4,128,384]{3,2,1,0:T(8,128)(2,1)}), bf16[8,4,128,384]{3,2,1,0:T(8,128)(2,1)S(1)}, u32[]{:S(2)}, u32[]{:S(2)}) async-start(bf16[8,4,128,384]{3,2,1,0:T(8,128)(2,1)} %get-tuple-element.39), calls=%async_computation.4 | async-start | bytes 6291456 | tf_op jit(solution)/shard_map/all_to_all | solution.py:402
  161.7 64.5 %reduce-scatter.5.cloned.1.call-start = ((), (), s32[]{:S(2)}) async-start(), calls=%async_computation.8 | async-start | bytes 491520 | tf_op jit(solution)/shard_map/reduce_scatter | solution.py:409
  161.8 12.5 %copy-start.10 = (s32[2,32]{1,0:T(2,128)S(1)}, s32[2,32]{1,0:T(2,128)}, u32[]{:S(2)}) copy-start(s32[2,32]{1,0:T(2,128)} %get-tuple-element.33) | copy-start | bytes 772
  200.6 44.7 %copy-start.9 = (bf16[128,32]{1,0:T(8,128)(2,1)S(1)}, bf16[128,32]{1,0:T(8,128)(2,1)}, u32[]{:S(2)}) copy-start(bf16[128,32]{1,0:T(8,128)(2,1)} %get-tuple-element.24) | copy-start | bytes 24580
  226.2 12.3 %all-to-all-start.1 = ((bf16[8,16,384]{2,1,0:T(8,128)(2,1)}), bf16[8,16,384]{2,1,0:T(8,128)(2,1)S(1)}, u32[]{:S(2)}, u32[]{:S(2)}) async-start(bf16[8,16,384]{2,1,0:T(8,128)(2,1)} %bitcast.40), calls=%async_computation.3 | async-start | bytes 196608 | tf_op jit(solution)/shard_map/all_to_all | solution.py:423
  238.6 15.7 %all-to-all-start.4 = ((bf16[8,32,384]{2,1,0:T(8,128)(2,1)}), bf16[8,32,384]{2,1,0:T(8,128)(2,1)S(1)}, u32[]{:S(2)}, u32[]{:S(2)}) async-start(bf16[8,32,384]{2,1,0:T(8,128)(2,1)} %bitcast.13), calls=%async_computation.6 | async-start | bytes 393216 | tf_op jit(solution)/shard_map/all_to_all | solution.py:415
  (1 other events, 1.1 us)
Sparse Core Ops, SparseCore 0:
  39.5 83.1 all-gather.4
  153.2 46.7 reduce-scatter.2
  202.5 23.7 reduce-scatter.4
